TPU v7x, 256 devices: a whole 4x4x8 slice. The times are simulated.
256 devices in a mesh: lat: 64 (over x, z, core), lev: 4 (over y).
Axes of the slice: x: 4, y: 4, z: 8, core: 2. Of those that a mesh axis runs over, the one named last changes fastest.
Arguments:
- field: bfloat16 [64, 1280, 2560], P('lev', 'lat'), may hold values from -6 to 6
- metric: float32 [3, 1280], P(None, 'lat'), may hold values from 0.3 to 3
- quad_weight: float32 [1280], replicated, may hold values from 0.5 to 2
- assignment: int32 [256, 5], replicated, may hold values from 0 to 1279, as said below
- legendre: bfloat16 [256, 3330, 1280], P(('lat', 'lev')), may hold values from -0.15625 to 0.15625
Outputs:
- solution: bfloat16 [64, 1280, 2560], P('lev', 'lat')
Inputs may be any that keep to these rules, and one draw needn't show every extreme that they name: `assignment`: every wavenumber 0 .. 1279 appears exactly once. Each row is one set: set s holds r * D + s for even rounds r and r * D + D - 1 - s for odd rounds r, in round order, with D the number of devices; the sets are dealt to the rows in an order drawn from the seed. So the total of (1280 - m) over a row is at most 3330, and one row reaches it.
All inputs are finite; a program needn't handle non-finite values.
Results may differ from a plain program's by a relative error of at most 0.0096.
Values may be sent and summed in bfloat16 or wider, within the bound.
No kernel may reach another device: no remote copies, remote signals or barrier semaphores. Data moves between devices by JAX's collectives and lax.ppermute only.
A program may use at most 192 MiB of HBM per device.

v0:
```python
import math

import jax
import jax.numpy as jnp
import numpy as np
from jax import lax
from jax.experimental import pallas as pl
from jax.experimental.pallas import tpu as pltpu
from jax.sharding import PartitionSpec as P

NLAT = 1280
NLON = 2560
HALF = NLON // 2
SLOTS = 5
SETS = 256
BAND = 20
LEVS = 16
ROWS = BAND * LEVS
MSG = 25
PITCH = 32
LAT_DEVS = 64
LEV_DEVS = 4
CAP = 3330
VMEM_LIMIT = 56 * 1024 * 1024
AXES = ("lev", "lat")


def set_waves():
    rounds = np.arange(SLOTS)[:, None]
    sets = np.arange(SETS)[None, :]
    return rounds * SETS + np.where(rounds % 2 == 0, sets, SETS - 1 - sets)


def trig(waves):
    phases = (np.arange(HALF, dtype=np.int64)[:, None] * waves[None, :]) % NLON
    angles = phases.astype(np.float64) * (2.0 * math.pi / NLON)
    return np.stack((np.cos(angles), -np.sin(angles)), axis=2) / math.sqrt(NLON)


def forward_table():
    waves = set_waves()
    table = np.zeros((SLOTS, 2, HALF, 2, SETS // 2), np.float32)
    for slot in range(SLOTS):
        for odd in range(2):
            table[slot, odd] = trig(waves[slot, odd::2]).transpose(0, 2, 1)
    return table.reshape(SLOTS, 2, HALF, SETS).astype(jnp.bfloat16)


def inverse_table():
    waves = set_waves()
    table = np.zeros((2, SLOTS, 2, SETS // 2, HALF), np.float32)
    for slot in range(SLOTS):
        for parity in range(2):
            chosen = waves[slot, (slot + parity) % 2 :: 2]
            scale = np.where(chosen == 0, 1.0, 2.0)
            table[parity, slot] = (trig(chosen) * scale[None, :, None]).transpose(2, 1, 0)
    table = table.reshape(2, HALF, SLOTS, SETS).transpose(2, 0, 1, 3)
    return np.ascontiguousarray(table).astype(jnp.bfloat16)


def block_exchange(tiles):
    lanes = lax.broadcasted_iota(jnp.int32, tiles[0].shape, 1)
    low = lanes < 64
    even = (lanes // 32) % 2 == 0
    mixed = [None] * 4
    for one in (0, 1):
        first, second = tiles[one], tiles[one + 2]
        mixed[one] = jnp.where(low, first, pltpu.roll(second, 64, 1))
        mixed[one + 2] = jnp.where(low, pltpu.roll(first, 64, 1), second)
    done = [None] * 4
    for one in (0, 2):
        first, second = mixed[one], mixed[one + 1]
        done[one] = jnp.where(even, first, pltpu.roll(second, 32, 1))
        done[one + 1] = jnp.where(even, pltpu.roll(first, 96, 1), second)
    return done


def send_kernel(
    metric_ref, quad_ref, field_ref, north_ref, south_ref, pick_ref, table_ref,
    out_ref, halves, mixed, rows,
):
    slot = pl.program_id(0)

    @pl.when(slot == 0)
    def _():
        def stencil(lat, centre, north, south):
            zonal = pltpu.roll(centre, 1, 1) + pltpu.roll(centre, NLON - 1, 1) - 2.0 * centre
            total = metric_ref[0, lat] * (north - centre) + metric_ref[1, lat] * (south - centre)
            total = total + metric_ref[2, lat] * zonal
            first, second = total[:, :HALF], total[:, HALF:]
            where = pl.ds(pl.multiple_of(lat * LEVS, LEVS), LEVS)
            halves[0, where, :] = (first + second).astype(jnp.bfloat16)
            halves[1, where, :] = (first - second).astype(jnp.bfloat16)

        def band(lat):
            return field_ref[pl.ds(pl.multiple_of(lat * LEVS, LEVS), LEVS), :].astype(jnp.float32)

        stencil(0, band(0), north_ref[...].astype(jnp.float32), band(1))
        stencil(
            BAND - 1, band(BAND - 1), band(BAND - 2), south_ref[...].astype(jnp.float32)
        )

        @pl.loop(1, BAND - 1)
        def _(lat):
            stencil(lat, band(lat), band(lat - 1), band(lat + 1))

    for odd in range(2):
        waves = jnp.dot(
            halves[(slot + odd) % 2], table_ref[0, odd], preferred_element_type=jnp.float32
        )
        for lat in range(BAND):
            weighted = (waves[lat * LEVS : (lat + 1) * LEVS] * quad_ref[lat]).astype(jnp.bfloat16)
            for part in range(2):
                start = (2 * lat + part) * LEVS
                mixed[start : start + LEVS, odd * 128 : odd * 128 + 128] = weighted[
                    :, part * 128 : part * 128 + 128
                ]
    dealt = lax.dot_general(
        pick_ref[...], mixed[...], (((1,), (1,)), ((), ())), preferred_element_type=jnp.float32
    )
    for part in range(5):
        rows[pl.ds(slot * 5 + part, SETS, stride=PITCH), :] = dealt[:, part * 128 : part * 128 + 128]

    @pl.when(slot == SLOTS - 1)
    def _():
        @pl.loop(0, SETS, step=8)
        def _(dest):
            for more in range(8):
                start = pl.multiple_of((dest + more) * PITCH, PITCH)
                out_ref[dest + more] = rows[pl.ds(start, PITCH), :].astype(jnp.bfloat16)[:MSG]


def send(metric, quad, field, north, south, pick, table):
    smem = pl.BlockSpec(memory_space=pltpu.SMEM)
    return pl.pallas_call(
        send_kernel,
        out_shape=jax.ShapeDtypeStruct((SETS, MSG, 128), jnp.bfloat16),
        grid=(SLOTS,),
        in_specs=[
            smem,
            smem,
            pl.BlockSpec((ROWS, NLON), lambda i: (0, 0)),
            pl.BlockSpec((LEVS, NLON), lambda i: (0, 0)),
            pl.BlockSpec((LEVS, NLON), lambda i: (0, 0)),
            pl.BlockSpec((SETS, SETS), lambda i: (0, 0)),
            pl.BlockSpec((1, 2, HALF, SETS), lambda i: (i, 0, 0, 0)),
        ],
        out_specs=pl.BlockSpec((SETS, MSG, 128), lambda i: (0, 0, 0)),
        scratch_shapes=[
            pltpu.VMEM((2, ROWS, HALF), jnp.bfloat16),
            pltpu.VMEM((2 * ROWS, SETS), jnp.bfloat16),
            pltpu.VMEM((SETS * PITCH, 128), jnp.float32),
        ],
        compiler_params=pltpu.CompilerParams(vmem_limit_bytes=VMEM_LIMIT),
        cost_estimate=pl.CostEstimate(flops=2_500_000_000, bytes_accessed=12_000_000, transcendentals=0),
        name="send",
    )(metric, quad, field, north, south, pick, table)


BLOCKS = [(0, 1), (0, 1), (0, 1), (0, 1), (0, 2), (1, 1), (1, 1), (1, 1), (1, 2), (2, 1), (2, 2), (2, 2), (3, 2)]


def spectral_kernel(set_ref, got_ref, legendre_ref, out_ref, rows, column, weighted, reduced, tail):
    number = set_ref[0]
    starts = (0, NLAT - number, 2049, 2817 - number, 3074, CAP - number)
    bases = (number, -769, number - 1537, -1794, number - 2050)

    @pl.loop(0, LEV_DEVS * LAT_DEVS, step=8)
    def _(source):
        for more in range(8):
            start = pl.multiple_of((source + more) * PITCH, PITCH)
            rows[pl.ds(start, MSG), :] = got_ref[source + more].astype(jnp.float32)

    for slot in range(SLOTS):
        for part in range(5):
            row = slot * 5 + part
            tiles = [
                rows[pl.ds(lev * LAT_DEVS * PITCH + row, LAT_DEVS, stride=PITCH), :]
                for lev in range(LEV_DEVS)
            ]
            for group, tile in enumerate(block_exchange(tiles)):
                column[pl.ds(4 * part + group, LAT_DEVS, stride=BAND), :] = tile
        weighted[:, slot * 128 : slot * 128 + 128] = column[...].astype(jnp.bfloat16)

    def damp(coeffs, first_row, slots):
        ids = lax.broadcasted_iota(jnp.int32, (coeffs.shape[0], 128), 0) + first_row
        pieces = []
        for place, slot in enumerate(slots):
            degree = (ids + bases[slot]).astype(jnp.float32)
            valid = (ids >= starts[slot]) & (ids < starts[slot + 1])
            bottom = 1.0 + degree * (degree + 1.0) * (4.0 / float(NLAT * NLAT))
            part = coeffs[:, place * 128 : place * 128 + 128]
            pieces.append(jnp.where(valid, part / bottom, 0.0))
        return pieces

    spans = [[None, 0] for _ in range(SLOTS)]
    for block, (first, count) in enumerate(BLOCKS):
        coeffs = jnp.dot(
            legendre_ref[0, block * 256 : block * 256 + 256, :],
            weighted[:, first * 128 : (first + count) * 128],
            preferred_element_type=jnp.float32,
        )
        slots = range(first, first + count)
        for slot, piece in zip(slots, damp(coeffs, block * 256, slots)):
            if spans[slot][0] is None:
                spans[slot][0] = block
            place = (block - spans[slot][0]) * 256
            spans[slot][1] = place + 256
            reduced[slot, :, place : place + 256] = piece.T.astype(jnp.bfloat16)
    tail[...] = jnp.zeros_like(tail)
    tail[0:2, :] = legendre_ref[0, 3328:3330, :]
    coeffs = jnp.dot(tail[...], weighted[:, 512:640], preferred_element_type=jnp.float32)
    last = jnp.concatenate(
        [damp(coeffs, 3328, (4,))[0], jnp.zeros((112, 128), jnp.float32)], axis=0
    ).T.astype(jnp.bfloat16)[:, :16]

    for slot in range(SLOTS):
        first, length = spans[slot]
        back = jnp.dot(
            reduced[slot, :, :length],
            legendre_ref[0, first * 256 : first * 256 + length, :],
            preferred_element_type=jnp.float32,
        )
        if slot == SLOTS - 1:
            back = back + jnp.dot(last, tail[...], preferred_element_type=jnp.float32)
        column[...] = back.T
        for part in range(5):
            tiles = [
                column[pl.ds(4 * part + group, LAT_DEVS, stride=BAND), :] for group in range(4)
            ]
            row = slot * 5 + part
            for lev, tile in enumerate(block_exchange(tiles)):
                rows[pl.ds(lev * LAT_DEVS * PITCH + row, LAT_DEVS, stride=PITCH), :] = tile

    @pl.loop(0, LEV_DEVS * LAT_DEVS, step=8)
    def _(dest):
        for more in range(8):
            start = pl.multiple_of((dest + more) * PITCH, PITCH)
            out_ref[dest + more] = rows[pl.ds(start, PITCH), :].astype(jnp.bfloat16)[:MSG]


def spectral(number, got, legendre):
    return pl.pallas_call(
        spectral_kernel,
        out_shape=jax.ShapeDtypeStruct((SETS, MSG, 128), jnp.bfloat16),
        in_specs=[
            pl.BlockSpec(memory_space=pltpu.SMEM),
            pl.BlockSpec(memory_space=pltpu.VMEM),
            pl.BlockSpec(memory_space=pltpu.VMEM),
        ],
        out_specs=pl.BlockSpec(memory_space=pltpu.VMEM),
        scratch_shapes=[
            pltpu.VMEM((SETS * PITCH, 128), jnp.float32),
            pltpu.VMEM((NLAT, 128), jnp.float32),
            pltpu.VMEM((NLAT, SLOTS * 128), jnp.bfloat16),
            pltpu.VMEM((SLOTS, 128, NLAT), jnp.bfloat16),
            pltpu.VMEM((16, NLAT), jnp.bfloat16),
        ],
        compiler_params=pltpu.CompilerParams(vmem_limit_bytes=VMEM_LIMIT),
        cost_estimate=pl.CostEstimate(flops=2_500_000_000, bytes_accessed=12_000_000, transcendentals=0),
        name="spectral",
    )(number, got, legendre)


def receive_kernel(got_ref, pick_ref, table_ref, out_ref, rows, waves):
    block = pl.program_id(0)

    @pl.when(block == 0)
    def _():
        @pl.loop(0, SETS, step=8)
        def _(source):
            for more in range(8):
                start = pl.multiple_of((source + more) * PITCH, PITCH)
                rows[pl.ds(start, MSG), :] = got_ref[source + more].astype(jnp.float32)

        for slot in range(SLOTS):
            for part in range(5):
                tile = rows[pl.ds(slot * 5 + part, SETS, stride=PITCH), :]
                dealt = jnp.dot(
                    tile.T.astype(jnp.bfloat16), pick_ref[...], preferred_element_type=jnp.float32
                ).astype(jnp.bfloat16)
                for group in range(8):
                    lat, side = 4 * part + group // 2, group % 2
                    for parity in range(2):
                        odd = (slot + parity) % 2
                        place = (2 * slot + side) * 128
                        waves[parity, lat * LEVS : lat * LEVS + LEVS, place : place + 128] = dealt[
                            group * LEVS : group * LEVS + LEVS, odd * 128 : odd * 128 + 128
                        ]

    even = jnp.dot(waves[0], table_ref[0, 0], preferred_element_type=jnp.float32)
    odd = jnp.dot(waves[1], table_ref[0, 1], preferred_element_type=jnp.float32)
    first = pl.multiple_of(block * SETS, SETS)
    out_ref[:, pl.ds(first, SETS)] = (even + odd).astype(jnp.bfloat16)
    second = pl.multiple_of(HALF + block * SETS, SETS)
    out_ref[:, pl.ds(second, SETS)] = (even - odd).astype(jnp.bfloat16)


def receive(got, pick, table):
    return pl.pallas_call(
        receive_kernel,
        out_shape=jax.ShapeDtypeStruct((ROWS, NLON), jnp.bfloat16),
        grid=(SLOTS,),
        in_specs=[
            pl.BlockSpec((SETS, MSG, 128), lambda i: (0, 0, 0)),
            pl.BlockSpec((SETS, SETS), lambda i: (0, 0)),
            pl.BlockSpec((1, 2, HALF, SETS), lambda i: (i, 0, 0, 0)),
        ],
        out_specs=pl.BlockSpec((ROWS, NLON), lambda i: (0, 0)),
        scratch_shapes=[
            pltpu.VMEM((SETS * PITCH, 128), jnp.float32),
            pltpu.VMEM((2, ROWS, HALF), jnp.bfloat16),
        ],
        compiler_params=pltpu.CompilerParams(vmem_limit_bytes=VMEM_LIMIT),
        cost_estimate=pl.CostEstimate(flops=2_500_000_000, bytes_accessed=12_000_000, transcendentals=0),
        name="receive",
    )(got, pick, table)


def pick_matrix(assignment):
    sets = assignment[:, 0].reshape(LAT_DEVS, LEV_DEVS).T.reshape(SETS)
    position = (sets % 2) * (SETS // 2) + sets // 2
    return (position[:, None] == jnp.arange(SETS, dtype=jnp.int32)[None, :]).astype(jnp.bfloat16)


def per_device(field, metric, quad_weight, assignment, legendre):
    lat_index = lax.axis_index("lat")
    device = lat_index * LEV_DEVS + lax.axis_index("lev")
    field = jnp.transpose(field, (1, 0, 2)).reshape(ROWS, NLON)
    forward = [(i, i + 1) for i in range(LAT_DEVS - 1)]
    backward = [(i + 1, i) for i in range(LAT_DEVS - 1)]
    north = lax.ppermute(field[ROWS - LEVS :], "lat", forward)
    south = lax.ppermute(field[:LEVS], "lat", backward)
    quad = lax.dynamic_slice_in_dim(quad_weight, lat_index * BAND, BAND, 0)
    number = lax.dynamic_slice_in_dim(assignment[:, 0], device, 1, 0)
    pick = pick_matrix(assignment)
    message = send(metric, quad, field, north, south, pick, forward_table())
    got = lax.all_to_all(message, AXES, split_axis=0, concat_axis=0, tiled=True)
    back = spectral(number, got, legendre)
    back = lax.all_to_all(back, AXES, split_axis=0, concat_axis=0, tiled=True)
    out = receive(back, pick, inverse_table())
    return jnp.transpose(out.reshape(BAND, LEVS, NLON), (1, 0, 2))


def solution(mesh):
    in_specs = (P("lev", "lat", None), P(None, "lat"), P(), P(), P(("lat", "lev"), None, None))
    out_specs = P("lev", "lat", None)
    return jax.shard_map(
        per_device, mesh=mesh, in_specs=in_specs, out_specs=out_specs, check_vma=False
    )
```

profile of v0, /device:TPU:1, one launch (start us, length us, event | category | flops | bytes accessed | tf_op | source)
XLA Modules:
  0.0 184.5 jit_solution(1064519327905996747)
XLA Ops:
  0.0 0.9 slice_bitcast_fusion
  0.9 5.1 %collective-permute-start.1 = (bf16[16,2560]{1,0:T(8,128)(2,1)S(1)}, bf16[16,2560]{1,0:T(8,128)(2,1)S(1)}, u32[]{:S(2)}, u32[]{:S(2)}) collective-permute-start(bf16[16,2560]{1,0:T(8,128)(2,1)S(1)} %get-tuple-element.5), channel_id=1, source_target_pairs={{4,0},{8,4},{12,8},{16,12},{20,16},{24,20},{28,24},{32,28},{36,32}... | collective-permute-start | bytes 245768 | tf_op jit(solution)/shard_map/ppermute | solution.py:333
  6.1 1.9 %collective-permute-start = (bf16[16,2560]{1,0:T(8,128)(2,1)S(1)}, bf16[16,2560]{1,0:T(8,128)(2,1)S(1)}, u32[]{:S(2)}, u32[]{:S(2)}) collective-permute-start(bf16[16,2560]{1,0:T(8,128)(2,1)S(1)} %get-tuple-element.6), channel_id=1, source_target_pairs={{0,4},{4,8},{8,12},{12,16},{16,20},{20,24},{24,28},{28,32},{32,36}... | collective-permute-start | bytes 245768 | tf_op jit(solution)/shard_map/ppermute | solution.py:332
  8.0 0.7 slice_reduce_fusion
  8.7 0.1 reshape_squeeze.3
  8.9 0.1 copy.8
  8.9 0.1 reshape.63
  9.0 0.8 fusion.pick_ref
  9.8 1.3 dynamic_slice.10.quad_ref
  11.1 0.0 collective-permute-done.1.south_ref
  11.1 0.0 copy-start.1
  11.1 0.0 collective-permute-done.north_ref
  11.1 0.0 copy-start.2
  11.2 0.6 copy-done.1
  11.8 0.0 copy-done.2
  11.8 12.7 %send.1 = bf16[256,25,128]{2,1,0:T(8,128)(2,1)} custom-call(f32[3,20]{1,0:T(4,128)} %metric_ref.1, f32[20]{0:T(128)} %dynamic_slice.10.quad_ref, bf16[320,2560]{1,0:T(8,128)(2,1)} %bitcast.13, bf16[16,2560]{1,0:T(8,128)(2,1)} %copy-done.2, bf16[16,2560]{1,0:T(8,128)(2,1)} %copy-done.1, bf16[256,256]{1,0:T(8,128)(2,1)} %fusion.pick_ref, ...), custom_call_target="tpu_custom_call" | custom-call | flops 2500000000 | bytes 12000000 | tf_op jit(solution)/shard_map/send/pallas_call | solution.py:135
  24.5 14.4 %all-to-all-start = ((bf16[256,25,128]{2,1,0:T(8,128)(2,1)}), bf16[256,25,128]{2,1,0:T(8,128)(2,1)S(1)}, u32[]{:S(2)}, u32[]{:S(2)}) async-start(bf16[256,25,128]{2,1,0:T(8,128)(2,1)} %send.1), calls=%async_computation | async-start | bytes 4194304 | tf_op jit(solution)/shard_map/all_to_all | solution.py:338
  38.9 0.6 constant_dynamic-slice_fusion
  39.5 54.2 %all-to-all-done.got_ref = bf16[256,25,128]{2,1,0:T(8,128)(2,1)S(1)} async-done(((bf16[256,25,128]{2,1,0:T(8,128)(2,1)}), bf16[256,25,128]{2,1,0:T(8,128)(2,1)S(1)}, u32[]{:S(2)}, u32[]{:S(2)}) %all-to-all-start) | async-done | bytes 1638432 | tf_op jit(solution)/shard_map/all_to_all | solution.py:338
  93.7 0.0 copy-start
  93.7 1.3 copy-done
  95.1 19.6 %spectral.1 = bf16[256,25,128]{2,1,0:T(8,128)(2,1)} custom-call(s32[1]{0:T(128)} %bitcast.set_ref, bf16[256,25,128]{2,1,0:T(8,128)(2,1)} %copy-done, bf16[1,3330,1280]{2,1,0:T(8,128)(2,1)} %legendre_ref.1), custom_call_target="tpu_custom_call" | custom-call | flops 2500000000 | bytes 12000000 | tf_op jit(solution)/shard_map/spectral/pallas_call | solution.py:243
  114.7 59.5 %all_to_all.10.got_ref = bf16[256,25,128]{2,1,0:T(8,128)(2,1)} all-to-all(bf16[256,25,128]{2,1,0:T(8,128)(2,1)} %spectral.1), channel_id=1, replica_groups=mesh['lat'=64,'lev'=4] {'lev','lat'}, dimensions={0} | all-to-all | bytes 3276800 | tf_op jit(solution)/shard_map/all_to_all | solution.py:340
  174.2 10.3 %receive.1 = bf16[320,2560]{1,0:T(8,128)(2,1)} custom-call(bf16[256,25,128]{2,1,0:T(8,128)(2,1)} %all_to_all.10.got_ref, bf16[256,256]{1,0:T(8,128)(2,1)} %fusion.pick_ref, bf16[5,2,1280,256]{3,2,1,0:T(8,128)(2,1)} %constant.52.clone.table_ref), custom_call_target="tpu_custom_call" | custom-call | flops 2500000000 | bytes 12000000 | tf_op jit(solution)/shard_map/receive/pallas_call | solution.py:300
  (1 shorter events, 0.0 us)
Async XLA Ops:
  0.9 10.2 %collective-permute-start.1 = (bf16[16,2560]{1,0:T(8,128)(2,1)S(1)}, bf16[16,2560]{1,0:T(8,128)(2,1)S(1)}, u32[]{:S(2)}, u32[]{:S(2)}) collective-permute-start(bf16[16,2560]{1,0:T(8,128)(2,1)S(1)} %get-tuple-element.5), channel_id=1, source_target_pairs={{4,0},{8,4},{12,8},{16,12},{20,16},{24,20},{28,24},{32,28},{36,32}... | collective-permute-start | bytes 245768 | tf_op jit(solution)/shard_map/ppermute | solution.py:333
  6.1 5.0 %collective-permute-start = (bf16[16,2560]{1,0:T(8,128)(2,1)S(1)}, bf16[16,2560]{1,0:T(8,128)(2,1)S(1)}, u32[]{:S(2)}, u32[]{:S(2)}) collective-permute-start(bf16[16,2560]{1,0:T(8,128)(2,1)S(1)} %get-tuple-element.6), channel_id=1, source_target_pairs={{0,4},{4,8},{8,12},{12,16},{16,20},{20,24},{24,28},{28,32},{32,36}... | collective-permute-start | bytes 245768 | tf_op jit(solution)/shard_map/ppermute | solution.py:332
  11.1 0.6 copy-start.1
  11.1 0.7 copy-start.2
  24.5 69.2 %all-to-all-start = ((bf16[256,25,128]{2,1,0:T(8,128)(2,1)}), bf16[256,25,128]{2,1,0:T(8,128)(2,1)S(1)}, u32[]{:S(2)}, u32[]{:S(2)}) async-start(bf16[256,25,128]{2,1,0:T(8,128)(2,1)} %send.1), calls=%async_computation | async-start | bytes 4194304 | tf_op jit(solution)/shard_map/all_to_all | solution.py:338
  93.7 1.3 copy-start
where the time goes:
time: 185 us; the launch traced here: 184 us
  blocking collectives  59.5 us (32%)
  waiting for transfers between devices  54.2 us (29%)
  Pallas kernels  42.7 us (23%)
  starting transfers between devices  21.4 us (12%)
  local copies, waits for them, and re-layouts  5.8 us (3%)
    all_to_all x1, blocking collectives, per_device(): back = lax.all_to_all(back, AXES, split_axis=0, concat_axis=0, tiled=True)  59.5 us
    all_to_all x1, waiting for transfers between devices, per_device(): got = lax.all_to_all(message, AXES, split_axis=0, concat_axis=0, tiled=True)  54.2 us
    pallas_call x1, Pallas kernels, spectral(): pl.pallas_call(spectral_kernel, out_shape=jax.ShapeDtypeStruct((SETS, MSG...  19.6 us
    all_to_all x1, starting transfers between devices, per_device(): got = lax.all_to_all(message, AXES, split_axis=0, concat_axis=0, tiled=True)  14.4 us
    pallas_call x1, Pallas kernels, send(): pl.pallas_call(send_kernel, out_shape=jax.ShapeDtypeStruct((SETS, MSG, 12...  12.7 us
    pallas_call x1, Pallas kernels, receive(): pl.pallas_call(receive_kernel, out_shape=jax.ShapeDtypeStruct((ROWS, NLON...  10.3 us
    ppermute x1, starting transfers between devices, per_device(): south = lax.ppermute(field[:LEVS], 'lat', backward)  5.15 us
  transfers between devices with their start and end apart: 3, of which 1 were waited for; matrix products, arithmetic and copies ran while one was open for 2% of the time, Pallas kernels for 0%

commit v1 on v0

--- a/solution.py
+++ b/solution.py
@@ -16,12 +16,13 @@
 BAND = 20
 LEVS = 16
 ROWS = BAND * LEVS
-MSG = 25
-PITCH = 32
+PITCH = 26
+MSG_ROWS = SETS * PITCH
 LAT_DEVS = 64
 LEV_DEVS = 4
 CAP = 3330
-VMEM_LIMIT = 56 * 1024 * 1024
+VMEM_LIMIT = 32 * 1024 * 1024
+SEND_LIMIT = 54 * 1024 * 1024
 AXES = ("lev", "lat")
 
 
@@ -73,6 +74,13 @@
         done[one] = jnp.where(even, first, pltpu.roll(second, 32, 1))
         done[one + 1] = jnp.where(even, pltpu.roll(first, 96, 1), second)
     return done
+
+
+def copy_rows(target, source):
+    @pl.loop(0, MSG_ROWS, step=256)
+    def _(start):
+        where = pl.ds(pl.multiple_of(start, 256), 256)
+        target[where, :] = source[where, :].astype(target.dtype)
 
 
 def send_kernel(
@@ -123,18 +131,14 @@
 
     @pl.when(slot == SLOTS - 1)
     def _():
-        @pl.loop(0, SETS, step=8)
-        def _(dest):
-            for more in range(8):
-                start = pl.multiple_of((dest + more) * PITCH, PITCH)
-                out_ref[dest + more] = rows[pl.ds(start, PITCH), :].astype(jnp.bfloat16)[:MSG]
+        copy_rows(out_ref, rows)
 
 
 def send(metric, quad, field, north, south, pick, table):
     smem = pl.BlockSpec(memory_space=pltpu.SMEM)
     return pl.pallas_call(
         send_kernel,
-        out_shape=jax.ShapeDtypeStruct((SETS, MSG, 128), jnp.bfloat16),
+        out_shape=jax.ShapeDtypeStruct((MSG_ROWS, 128), jnp.bfloat16),
         grid=(SLOTS,),
         in_specs=[
             smem,
@@ -145,13 +149,13 @@
             pl.BlockSpec((SETS, SETS), lambda i: (0, 0)),
             pl.BlockSpec((1, 2, HALF, SETS), lambda i: (i, 0, 0, 0)),
         ],
-        out_specs=pl.BlockSpec((SETS, MSG, 128), lambda i: (0, 0, 0)),
+        out_specs=pl.BlockSpec((MSG_ROWS, 128), lambda i: (0, 0)),
         scratch_shapes=[
             pltpu.VMEM((2, ROWS, HALF), jnp.bfloat16),
             pltpu.VMEM((2 * ROWS, SETS), jnp.bfloat16),
-            pltpu.VMEM((SETS * PITCH, 128), jnp.float32),
-        ],
-        compiler_params=pltpu.CompilerParams(vmem_limit_bytes=VMEM_LIMIT),
+            pltpu.VMEM((MSG_ROWS, 128), jnp.float32),
+        ],
+        compiler_params=pltpu.CompilerParams(vmem_limit_bytes=SEND_LIMIT),
         cost_estimate=pl.CostEstimate(flops=2_500_000_000, bytes_accessed=12_000_000, transcendentals=0),
         name="send",
     )(metric, quad, field, north, south, pick, table)
@@ -165,11 +169,7 @@
     starts = (0, NLAT - number, 2049, 2817 - number, 3074, CAP - number)
     bases = (number, -769, number - 1537, -1794, number - 2050)
 
-    @pl.loop(0, LEV_DEVS * LAT_DEVS, step=8)
-    def _(source):
-        for more in range(8):
-            start = pl.multiple_of((source + more) * PITCH, PITCH)
-            rows[pl.ds(start, MSG), :] = got_ref[source + more].astype(jnp.float32)
+    copy_rows(rows, got_ref)
 
     for slot in range(SLOTS):
         for part in range(5):
@@ -232,17 +232,13 @@
             for lev, tile in enumerate(block_exchange(tiles)):
                 rows[pl.ds(lev * LAT_DEVS * PITCH + row, LAT_DEVS, stride=PITCH), :] = tile
 
-    @pl.loop(0, LEV_DEVS * LAT_DEVS, step=8)
-    def _(dest):
-        for more in range(8):
-            start = pl.multiple_of((dest + more) * PITCH, PITCH)
-            out_ref[dest + more] = rows[pl.ds(start, PITCH), :].astype(jnp.bfloat16)[:MSG]
+    copy_rows(out_ref, rows)
 
 
 def spectral(number, got, legendre):
     return pl.pallas_call(
         spectral_kernel,
-        out_shape=jax.ShapeDtypeStruct((SETS, MSG, 128), jnp.bfloat16),
+        out_shape=jax.ShapeDtypeStruct((MSG_ROWS, 128), jnp.bfloat16),
         in_specs=[
             pl.BlockSpec(memory_space=pltpu.SMEM),
             pl.BlockSpec(memory_space=pltpu.VMEM),
@@ -250,7 +246,7 @@
         ],
         out_specs=pl.BlockSpec(memory_space=pltpu.VMEM),
         scratch_shapes=[
-            pltpu.VMEM((SETS * PITCH, 128), jnp.float32),
+            pltpu.VMEM((MSG_ROWS, 128), jnp.float32),
             pltpu.VMEM((NLAT, 128), jnp.float32),
             pltpu.VMEM((NLAT, SLOTS * 128), jnp.bfloat16),
             pltpu.VMEM((SLOTS, 128, NLAT), jnp.bfloat16),
@@ -267,11 +263,7 @@
 
     @pl.when(block == 0)
     def _():
-        @pl.loop(0, SETS, step=8)
-        def _(source):
-            for more in range(8):
-                start = pl.multiple_of((source + more) * PITCH, PITCH)
-                rows[pl.ds(start, MSG), :] = got_ref[source + more].astype(jnp.float32)
+        copy_rows(rows, got_ref)
 
         for slot in range(SLOTS):
             for part in range(5):
@@ -302,13 +294,13 @@
         out_shape=jax.ShapeDtypeStruct((ROWS, NLON), jnp.bfloat16),
         grid=(SLOTS,),
         in_specs=[
-            pl.BlockSpec((SETS, MSG, 128), lambda i: (0, 0, 0)),
+            pl.BlockSpec((MSG_ROWS, 128), lambda i: (0, 0)),
             pl.BlockSpec((SETS, SETS), lambda i: (0, 0)),
             pl.BlockSpec((1, 2, HALF, SETS), lambda i: (i, 0, 0, 0)),
         ],
         out_specs=pl.BlockSpec((ROWS, NLON), lambda i: (0, 0)),
         scratch_shapes=[
-            pltpu.VMEM((SETS * PITCH, 128), jnp.float32),
+            pltpu.VMEM((MSG_ROWS, 128), jnp.float32),
             pltpu.VMEM((2, ROWS, HALF), jnp.bfloat16),
         ],
         compiler_params=pltpu.CompilerParams(vmem_limit_bytes=VMEM_LIMIT),
@@ -321,6 +313,11 @@
     sets = assignment[:, 0].reshape(LAT_DEVS, LEV_DEVS).T.reshape(SETS)
     position = (sets % 2) * (SETS // 2) + sets // 2
     return (position[:, None] == jnp.arange(SETS, dtype=jnp.int32)[None, :]).astype(jnp.bfloat16)
+
+
+def exchange(message):
+    pairs = message.reshape(SETS, PITCH // 2, 2, 128)
+    return lax.all_to_all(pairs, AXES, split_axis=0, concat_axis=0, tiled=True).reshape(MSG_ROWS, 128)
 
 
 def per_device(field, metric, quad_weight, assignment, legendre):
@@ -334,10 +331,9 @@
     quad = lax.dynamic_slice_in_dim(quad_weight, lat_index * BAND, BAND, 0)
     number = lax.dynamic_slice_in_dim(assignment[:, 0], device, 1, 0)
     pick = pick_matrix(assignment)
+    number, quad, pick, north, south = lax.optimization_barrier((number, quad, pick, north, south))
     message = send(metric, quad, field, north, south, pick, forward_table())
-    got = lax.all_to_all(message, AXES, split_axis=0, concat_axis=0, tiled=True)
-    back = spectral(number, got, legendre)
-    back = lax.all_to_all(back, AXES, split_axis=0, concat_axis=0, tiled=True)
+    back = exchange(spectral(number, exchange(message), legendre))
     out = receive(back, pick, inverse_table())
     return jnp.transpose(out.reshape(BAND, LEVS, NLON), (1, 0, 2))
 

time: 185 us -> 151 us (0.82)
  waiting for transfers between devices: 54.2 us -> 0.01 us
  blocking collectives: 59.5 us -> 112 us
  Pallas kernels: 42.7 us -> 26.8 us
  starting transfers between devices: 21.4 us -> 7.07 us
    all_to_all x1 -> x0, waiting for transfers between devices: 54.2 us -> none  [per_device(): got = lax.all_to_all(message, AXES, split_axis=0, concat_axis=0, tiled=True)]
    all_to_all x1 -> x2, blocking collectives: 59.5 us -> 112 us  [exchange(): lax.all_to_all(pairs, AXES, split_axis=0, concat_axis=0, tiled=True)]
    all_to_all x1 -> x0, starting transfers between devices: 14.4 us -> none  [per_device(): got = lax.all_to_all(message, AXES, split_axis=0, concat_axis=0, tiled=True)]
    pallas_call x2, Pallas kernels: 32.4 us -> 21.6 us  [the longest x1 11.6 us: send(): pl.pallas_call(send_kernel, out_shape=jax.ShapeDtypeStruct((MSG_ROWS, 128...]
    pallas_call x1, Pallas kernels: 10.3 us -> 5.21 us  [receive(): pl.pallas_call(receive_kernel, out_shape=jax.ShapeDtypeStruct((ROWS, NLON...]
  transfers between devices with their start and end apart: 3 -> 2, of which waited for: 1 -> 0; matrix products, arithmetic and copies ran while one was open for 2% -> 2% of each run, Pallas kernels for 0% -> 0%
where the time goes in v1:
time: 151 us
  blocking collectives  112 us (74%)
  Pallas kernels  26.8 us (18%)
  starting transfers between devices  7.07 us (5%)
  local copies, waits for them, and re-layouts  4.47 us (3%)
    all_to_all x2, blocking collectives, exchange(): lax.all_to_all(pairs, AXES, split_axis=0, concat_axis=0, tiled=True)  112 us
    pallas_call x1, Pallas kernels, send(): pl.pallas_call(send_kernel, out_shape=jax.ShapeDtypeStruct((MSG_ROWS, 128...  11.6 us
    pallas_call x1, Pallas kernels, spectral(): pl.pallas_call(spectral_kernel, out_shape=jax.ShapeDtypeStruct((MSG_ROWS,...  9.98 us
    pallas_call x1, Pallas kernels, receive(): pl.pallas_call(receive_kernel, out_shape=jax.ShapeDtypeStruct((ROWS, NLON...  5.21 us
    ppermute x1, starting transfers between devices, per_device(): south = lax.ppermute(field[:LEVS], 'lat', backward)  5.15 us
  transfers between devices with their start and end apart: 2, of which 0 were waited for; matrix products, arithmetic and copies ran while one was open for 2% of the time, Pallas kernels for 0%

profile of v1, /device:TPU:1, one launch (start us, length us, event | category | flops | bytes accessed | tf_op | source)
XLA Modules:
  0.0 150.9 jit_solution(1262733698589604670)
XLA Ops:
  0.0 0.9 slice_bitcast_fusion
  0.9 5.1 %collective-permute-start.1 = (bf16[16,2560]{1,0:T(8,128)(2,1)S(1)}, bf16[16,2560]{1,0:T(8,128)(2,1)S(1)}, u32[]{:S(2)}, u32[]{:S(2)}) collective-permute-start(bf16[16,2560]{1,0:T(8,128)(2,1)S(1)} %get-tuple-element.15), channel_id=1, source_target_pairs={{4,0},{8,4},{12,8},{16,12},{20,16},{24,20},{28,24},{32,28},{36,32}... | collective-permute-start | bytes 245768 | tf_op jit(solution)/shard_map/ppermute | solution.py:330
  6.1 1.9 %collective-permute-start = (bf16[16,2560]{1,0:T(8,128)(2,1)S(1)}, bf16[16,2560]{1,0:T(8,128)(2,1)S(1)}, u32[]{:S(2)}, u32[]{:S(2)}) collective-permute-start(bf16[16,2560]{1,0:T(8,128)(2,1)S(1)} %get-tuple-element.16), channel_id=1, source_target_pairs={{0,4},{4,8},{8,12},{12,16},{16,20},{20,24},{24,28},{28,32},{32,36}... | collective-permute-start | bytes 245768 | tf_op jit(solution)/shard_map/ppermute | solution.py:329
  8.0 0.7 slice_reduce_fusion
  8.7 0.1 reshape_squeeze.3
  8.9 0.1 copy.8
  8.9 0.1 reshape.74
  9.0 0.8 fusion.pick_ref
  9.8 1.2 dynamic_slice.10.quad_ref
  11.0 0.6 constant_dynamic-slice_fusion
  11.7 0.0 collective-permute-done.1.south_ref
  11.7 0.0 copy-start.2
  11.7 0.0 collective-permute-done.north_ref
  11.7 0.0 copy-start.3
  11.7 0.6 copy-done.2
  12.3 0.0 copy-done.3
  12.4 0.0 copy-start
  12.4 11.6 %send.1 = bf16[6656,128]{1,0:T(8,128)(2,1)} custom-call(f32[3,20]{1,0:T(4,128)} %metric_ref.1, f32[20]{0:T(128)} %dynamic_slice.10.quad_ref, bf16[320,2560]{1,0:T(8,128)(2,1)} %bitcast.23, bf16[16,2560]{1,0:T(8,128)(2,1)} %copy-done.3, bf16[16,2560]{1,0:T(8,128)(2,1)} %copy-done.2, bf16[256,256]{1,0:T(8,128)(2,1)} %fusion.pick_ref, ...), custom_call_target="tpu_custom_call" | custom-call | flops 2500000000 | bytes 12000000 | tf_op jit(solution)/shard_map/send/pallas_call | solution.py:139
  24.0 0.0 slice-start
  24.0 60.9 %all_to_all.10 = bf16[256,13,2,128]{3,2,1,0:T(2,128)(2,1)S(1)} all-to-all(bf16[256,13,2,128]{3,2,1,0:T(2,128)(2,1)} %bitcast.21), channel_id=1, replica_groups=mesh['lat'=64,'lev'=4] {'lev','lat'}, dimensions={0} | all-to-all | bytes 3407872 | tf_op jit(solution)/shard_map/all_to_all | solution.py:320
  84.9 0.0 copy-done
  84.9 0.0 slice-start.1
  84.9 10.0 %spectral.1 = bf16[6656,128]{1,0:T(8,128)(2,1)S(1)} custom-call(s32[1]{0:T(128)} %bitcast.set_ref, bf16[6656,128]{1,0:T(8,128)(2,1)S(1)} %bitcast.17, bf16[1,3330,1280]{2,1,0:T(8,128)(2,1)S(1)} %copy-done), custom_call_target="tpu_custom_call" | custom-call | flops 2500000000 | bytes 12000000 | tf_op jit(solution)/shard_map/spectral/pallas_call | solution.py:239
  94.9 0.0 copy-start.1
  94.9 50.8 %all_to_all.11 = bf16[256,13,2,128]{3,2,1,0:T(2,128)(2,1)S(1)} all-to-all(bf16[256,13,2,128]{3,2,1,0:T(2,128)(2,1)S(1)} %bitcast.18), channel_id=1, replica_groups=mesh['lat'=64,'lev'=4] {'lev','lat'}, dimensions={0} | all-to-all | bytes 3407872 | tf_op jit(solution)/shard_map/all_to_all | solution.py:320
  145.7 0.0 slice-done
  145.7 0.0 slice-done.1
  145.7 0.0 copy-done.1
  145.7 5.2 %receive.1 = bf16[320,2560]{1,0:T(8,128)(2,1)} custom-call(bf16[6656,128]{1,0:T(8,128)(2,1)S(1)} %bitcast.16, bf16[256,256]{1,0:T(8,128)(2,1)S(1)} %copy-done.1, bf16[5,2,1280,256]{3,2,1,0:T(8,128)(2,1)S(1)} %bitcast.20), custom_call_target="tpu_custom_call" | custom-call | flops 2500000000 | bytes 12000000 | tf_op jit(solution)/shard_map/receive/pallas_call | solution.py:292
  (2 shorter events, 0.0 us)
Async XLA Ops:
  0.9 10.8 %collective-permute-start.1 = (bf16[16,2560]{1,0:T(8,128)(2,1)S(1)}, bf16[16,2560]{1,0:T(8,128)(2,1)S(1)}, u32[]{:S(2)}, u32[]{:S(2)}) collective-permute-start(bf16[16,2560]{1,0:T(8,128)(2,1)S(1)} %get-tuple-element.15), channel_id=1, source_target_pairs={{4,0},{8,4},{12,8},{16,12},{20,16},{24,20},{28,24},{32,28},{36,32}... | collective-permute-start | bytes 245768 | tf_op jit(solution)/shard_map/ppermute | solution.py:330
  6.1 5.6 %collective-permute-start = (bf16[16,2560]{1,0:T(8,128)(2,1)S(1)}, bf16[16,2560]{1,0:T(8,128)(2,1)S(1)}, u32[]{:S(2)}, u32[]{:S(2)}) collective-permute-start(bf16[16,2560]{1,0:T(8,128)(2,1)S(1)} %get-tuple-element.16), channel_id=1, source_target_pairs={{0,4},{4,8},{8,12},{12,16},{16,20},{20,24},{24,28},{28,32},{32,36}... | collective-permute-start | bytes 245768 | tf_op jit(solution)/shard_map/ppermute | solution.py:329
  11.7 0.6 copy-start.2
  11.7 0.7 copy-start.3
  12.4 72.5 %copy-start = (bf16[1,3330,1280]{2,1,0:T(8,128)(2,1)S(1)}, bf16[1,3330,1280]{2,1,0:T(8,128)(2,1)}, u32[]{:S(2)}) copy-start(bf16[1,3330,1280]{2,1,0:T(8,128)(2,1)} %legendre_ref.1) | copy-start | bytes 25574404
  24.0 121.7 %slice-start = ((s8[6553600]{0:T(1024)(128)(4,1)}), s8[4194304]{0:T(1024)(128)(4,1)S(1)}, s32[]{:S(2)}) async-start(s8[6553600]{0:T(1024)(128)(4,1)} %bitcast.19), calls=%async_computation.2 | async-start | bytes 8388608
  84.9 60.8 %slice-start.1 = ((s8[6553600]{0:T(1024)(128)(4,1)}), s8[2359296]{0:T(1024)(128)(4,1)S(1)}, s32[]{:S(2)}) async-start(s8[6553600]{0:T(1024)(128)(4,1)} %bitcast.19), calls=%async_computation.3 | async-start | bytes 4718592
  94.9 50.8 %copy-start.1 = (bf16[256,256]{1,0:T(8,128)(2,1)S(1)}, bf16[256,256]{1,0:T(8,128)(2,1)}, u32[]{:S(2)}) copy-start(bf16[256,256]{1,0:T(8,128)(2,1)} %fusion.pick_ref) | copy-start | bytes 393220

commit v2 on v1

--- a/solution.py
+++ b/solution.py
@@ -22,7 +22,8 @@
 LEV_DEVS = 4
 CAP = 3330
 VMEM_LIMIT = 32 * 1024 * 1024
-SEND_LIMIT = 54 * 1024 * 1024
+SEND_LIMIT = 48 * 1024 * 1024
+STENCIL_LIMIT = 16 * 1024 * 1024
 AXES = ("lev", "lat")
 
 
@@ -83,41 +84,88 @@
         target[where, :] = source[where, :].astype(target.dtype)
 
 
+def stencil_kernel(metric_ref, field_ref, halves_ref, edges_ref):
+    def band(lat):
+        return field_ref[pl.ds(pl.multiple_of(lat * LEVS, LEVS), LEVS), :].astype(jnp.float32)
+
+    def stencil(lat, north, south):
+        centre = band(lat)
+        zonal = pltpu.roll(centre, 1, 1) + pltpu.roll(centre, NLON - 1, 1) - 2.0 * centre
+        toward = -centre if north is None else north - centre
+        away = -centre if south is None else south - centre
+        total = metric_ref[0, lat] * toward + metric_ref[1, lat] * away
+        total = total + metric_ref[2, lat] * zonal
+        return total[:, :HALF] + total[:, HALF:], total[:, :HALF] - total[:, HALF:]
+
+    edges_ref[0, 0], edges_ref[0, 1] = stencil(0, None, band(1))
+    edges_ref[1, 0], edges_ref[1, 1] = stencil(BAND - 1, band(BAND - 2), None)
+
+    @pl.loop(1, BAND - 1)
+    def _(lat):
+        both = stencil(lat, band(lat - 1), band(lat + 1))
+        where = pl.ds(pl.multiple_of(lat * LEVS, LEVS), LEVS)
+        halves_ref[0, where, :] = both[0].astype(jnp.bfloat16)
+        halves_ref[1, where, :] = both[1].astype(jnp.bfloat16)
+
+
+def stencil(metric, field):
+    vmem = pl.BlockSpec(memory_space=pltpu.VMEM)
+    return pl.pallas_call(
+        stencil_kernel,
+        out_shape=(
+            jax.ShapeDtypeStruct((2, ROWS, HALF), jnp.bfloat16),
+            jax.ShapeDtypeStruct((2, 2, LEVS, HALF), jnp.float32),
+        ),
+        in_specs=[pl.BlockSpec(memory_space=pltpu.SMEM), vmem],
+        out_specs=(vmem, vmem),
+        compiler_params=pltpu.CompilerParams(vmem_limit_bytes=STENCIL_LIMIT),
+        cost_estimate=pl.CostEstimate(flops=20_000_000, bytes_accessed=4_000_000, transcendentals=0),
+        name="stencil",
+    )(metric, field)
+
+
 def send_kernel(
-    metric_ref, quad_ref, field_ref, north_ref, south_ref, pick_ref, table_ref,
-    out_ref, halves, mixed, rows,
+    metric_ref, quad_ref, sets_ref, part_ref, edges_ref, north_ref, south_ref, table_ref,
+    out_ref, pick_ref, halves, mixed, rows, picks, tables, landed,
 ):
     slot = pl.program_id(0)
 
+    def fetch(which):
+        return pltpu.make_async_copy(table_ref.at[which], tables.at[which], landed.at[which])
+
     @pl.when(slot == 0)
     def _():
-        def stencil(lat, centre, north, south):
-            zonal = pltpu.roll(centre, 1, 1) + pltpu.roll(centre, NLON - 1, 1) - 2.0 * centre
-            total = metric_ref[0, lat] * (north - centre) + metric_ref[1, lat] * (south - centre)
-            total = total + metric_ref[2, lat] * zonal
-            first, second = total[:, :HALF], total[:, HALF:]
-            where = pl.ds(pl.multiple_of(lat * LEVS, LEVS), LEVS)
-            halves[0, where, :] = (first + second).astype(jnp.bfloat16)
-            halves[1, where, :] = (first - second).astype(jnp.bfloat16)
-
-        def band(lat):
-            return field_ref[pl.ds(pl.multiple_of(lat * LEVS, LEVS), LEVS), :].astype(jnp.float32)
-
-        stencil(0, band(0), north_ref[...].astype(jnp.float32), band(1))
-        stencil(
-            BAND - 1, band(BAND - 1), band(BAND - 2), south_ref[...].astype(jnp.float32)
-        )
-
-        @pl.loop(1, BAND - 1)
-        def _(lat):
-            stencil(lat, band(lat), band(lat - 1), band(lat + 1))
-
+        for which in range(SLOTS):
+            fetch(which).start()
+        for edge, (lat, halo) in enumerate(((0, north_ref), (BAND - 1, south_ref))):
+            value = halo[...].astype(jnp.float32) * metric_ref[edge, lat]
+            first, second = value[:, :HALF], value[:, HALF:]
+            where = slice(lat * LEVS, (lat + 1) * LEVS)
+            halves[0, where, :] = (edges_ref[edge, 0] + (first + second)).astype(jnp.bfloat16)
+            halves[1, where, :] = (edges_ref[edge, 1] + (first - second)).astype(jnp.bfloat16)
+        inner = slice(LEVS, ROWS - LEVS)
+        halves[:, inner, :] = part_ref[:, inner, :]
+
+        sets = sets_ref[0:1, :]
+        position = (sets % 2) * (SETS // 2) + sets // 2
+        spots = lax.broadcasted_iota(jnp.int32, (SETS, SETS), 0)
+        for odd in range(2):
+            one_hot = jnp.where(spots[odd * 128 : odd * 128 + 128] == position, 1.0, 0.0)
+            picks[...] = one_hot.T
+            for lev in range(LEV_DEVS):
+                pick_ref[lev * LAT_DEVS : (lev + 1) * LAT_DEVS, odd * 128 : odd * 128 + 128] = picks[
+                    pl.ds(lev, LAT_DEVS, stride=LEV_DEVS), :
+                ].astype(jnp.bfloat16)
+
+    first_lat = lax.axis_index("lat") * BAND
+    fetch(slot).wait()
     for odd in range(2):
         waves = jnp.dot(
-            halves[(slot + odd) % 2], table_ref[0, odd], preferred_element_type=jnp.float32
+            halves[(slot + odd) % 2], tables[slot, odd], preferred_element_type=jnp.float32
         )
         for lat in range(BAND):
-            weighted = (waves[lat * LEVS : (lat + 1) * LEVS] * quad_ref[lat]).astype(jnp.bfloat16)
+            weight = quad_ref[first_lat + lat]
+            weighted = (waves[lat * LEVS : (lat + 1) * LEVS] * weight).astype(jnp.bfloat16)
             for part in range(2):
                 start = (2 * lat + part) * LEVS
                 mixed[start : start + LEVS, odd * 128 : odd * 128 + 128] = weighted[
@@ -134,38 +182,49 @@
         copy_rows(out_ref, rows)
 
 
-def send(metric, quad, field, north, south, pick, table):
+def send(metric, quad, sets, part, edges, north, south, table):
     smem = pl.BlockSpec(memory_space=pltpu.SMEM)
+
+    def whole(*shape):
+        return pl.BlockSpec(shape, lambda i: (0,) * len(shape))
+
     return pl.pallas_call(
         send_kernel,
-        out_shape=jax.ShapeDtypeStruct((MSG_ROWS, 128), jnp.bfloat16),
+        out_shape=(
+            jax.ShapeDtypeStruct((MSG_ROWS, 128), jnp.bfloat16),
+            jax.ShapeDtypeStruct((SETS, SETS), jnp.bfloat16),
+        ),
         grid=(SLOTS,),
         in_specs=[
             smem,
             smem,
-            pl.BlockSpec((ROWS, NLON), lambda i: (0, 0)),
-            pl.BlockSpec((LEVS, NLON), lambda i: (0, 0)),
-            pl.BlockSpec((LEVS, NLON), lambda i: (0, 0)),
-            pl.BlockSpec((SETS, SETS), lambda i: (0, 0)),
-            pl.BlockSpec((1, 2, HALF, SETS), lambda i: (i, 0, 0, 0)),
-        ],
-        out_specs=pl.BlockSpec((MSG_ROWS, 128), lambda i: (0, 0)),
+            whole(SLOTS, SETS),
+            whole(2, ROWS, HALF),
+            whole(2, 2, LEVS, HALF),
+            whole(LEVS, NLON),
+            whole(LEVS, NLON),
+            pl.BlockSpec(memory_space=pltpu.HBM),
+        ],
+        out_specs=(whole(MSG_ROWS, 128), whole(SETS, SETS)),
         scratch_shapes=[
             pltpu.VMEM((2, ROWS, HALF), jnp.bfloat16),
             pltpu.VMEM((2 * ROWS, SETS), jnp.bfloat16),
             pltpu.VMEM((MSG_ROWS, 128), jnp.float32),
+            pltpu.VMEM((SETS, 128), jnp.float32),
+            pltpu.VMEM((SLOTS, 2, HALF, SETS), jnp.bfloat16),
+            pltpu.SemaphoreType.DMA((SLOTS,)),
         ],
         compiler_params=pltpu.CompilerParams(vmem_limit_bytes=SEND_LIMIT),
         cost_estimate=pl.CostEstimate(flops=2_500_000_000, bytes_accessed=12_000_000, transcendentals=0),
         name="send",
-    )(metric, quad, field, north, south, pick, table)
+    )(metric, quad, sets, part, edges, north, south, table)
 
 
 BLOCKS = [(0, 1), (0, 1), (0, 1), (0, 1), (0, 2), (1, 1), (1, 1), (1, 1), (1, 2), (2, 1), (2, 2), (2, 2), (3, 2)]
 
 
-def spectral_kernel(set_ref, got_ref, legendre_ref, out_ref, rows, column, weighted, reduced, tail):
-    number = set_ref[0]
+def spectral_kernel(sets_ref, got_ref, legendre_ref, out_ref, rows, column, weighted, reduced, tail):
+    number = sets_ref[0, lax.axis_index("lat") * LEV_DEVS + lax.axis_index("lev")]
     starts = (0, NLAT - number, 2049, 2817 - number, 3074, CAP - number)
     bases = (number, -769, number - 1537, -1794, number - 2050)
 
@@ -235,7 +294,7 @@
     copy_rows(out_ref, rows)
 
 
-def spectral(number, got, legendre):
+def spectral(sets, got, legendre):
     return pl.pallas_call(
         spectral_kernel,
         out_shape=jax.ShapeDtypeStruct((MSG_ROWS, 128), jnp.bfloat16),
@@ -255,7 +314,7 @@
         compiler_params=pltpu.CompilerParams(vmem_limit_bytes=VMEM_LIMIT),
         cost_estimate=pl.CostEstimate(flops=2_500_000_000, bytes_accessed=12_000_000, transcendentals=0),
         name="spectral",
-    )(number, got, legendre)
+    )(sets, got, legendre)
 
 
 def receive_kernel(got_ref, pick_ref, table_ref, out_ref, rows, waves):
@@ -309,31 +368,21 @@
     )(got, pick, table)
 
 
-def pick_matrix(assignment):
-    sets = assignment[:, 0].reshape(LAT_DEVS, LEV_DEVS).T.reshape(SETS)
-    position = (sets % 2) * (SETS // 2) + sets // 2
-    return (position[:, None] == jnp.arange(SETS, dtype=jnp.int32)[None, :]).astype(jnp.bfloat16)
-
-
 def exchange(message):
     pairs = message.reshape(SETS, PITCH // 2, 2, 128)
     return lax.all_to_all(pairs, AXES, split_axis=0, concat_axis=0, tiled=True).reshape(MSG_ROWS, 128)
 
 
 def per_device(field, metric, quad_weight, assignment, legendre):
-    lat_index = lax.axis_index("lat")
-    device = lat_index * LEV_DEVS + lax.axis_index("lev")
     field = jnp.transpose(field, (1, 0, 2)).reshape(ROWS, NLON)
     forward = [(i, i + 1) for i in range(LAT_DEVS - 1)]
     backward = [(i + 1, i) for i in range(LAT_DEVS - 1)]
     north = lax.ppermute(field[ROWS - LEVS :], "lat", forward)
     south = lax.ppermute(field[:LEVS], "lat", backward)
-    quad = lax.dynamic_slice_in_dim(quad_weight, lat_index * BAND, BAND, 0)
-    number = lax.dynamic_slice_in_dim(assignment[:, 0], device, 1, 0)
-    pick = pick_matrix(assignment)
-    number, quad, pick, north, south = lax.optimization_barrier((number, quad, pick, north, south))
-    message = send(metric, quad, field, north, south, pick, forward_table())
-    back = exchange(spectral(number, exchange(message), legendre))
+    part, edges = stencil(metric, field)
+    sets = assignment.T
+    message, pick = send(metric, quad_weight, sets, part, edges, north, south, forward_table())
+    back = exchange(spectral(sets, exchange(message), legendre))
     out = receive(back, pick, inverse_table())
     return jnp.transpose(out.reshape(BAND, LEVS, NLON), (1, 0, 2))
 

time: 151 us -> 148 us (0.980)
    dynamic_slice x2 -> x0, local copies, waits for them, and re-layouts: 1.89 us -> none  [the longest x1 1.25 us: per_device(): quad = lax.dynamic_slice_in_dim(quad_weight, lat_index * BAND, BAND, 0)]
    pallas_call x1 -> x2, Pallas kernels: 11.6 us -> 10.5 us  [the longest x1 7.13 us: send(): pl.pallas_call(send_kernel, out_shape=(jax.ShapeDtypeStruct((MSG_ROWS, 12...]
  transfers between devices with their start and end apart: 2 -> 2, of which waited for: 0 -> 0; matrix products, arithmetic and copies ran while one was open for 2% -> 0% of each run, Pallas kernels for 0% -> 2%
where the time goes in v2:
time: 148 us
  blocking collectives  111 us (75%)
  Pallas kernels  25.8 us (17%)
  starting transfers between devices  7.07 us (5%)
  local copies, waits for them, and re-layouts  3.11 us (2%)
    all_to_all x2, blocking collectives, exchange(): lax.all_to_all(pairs, AXES, split_axis=0, concat_axis=0, tiled=True)  111 us
    pallas_call x1, Pallas kernels, spectral(): pl.pallas_call(spectral_kernel, out_shape=jax.ShapeDtypeStruct((MSG_ROWS,...  10.2 us
    pallas_call x1, Pallas kernels, send(): pl.pallas_call(send_kernel, out_shape=(jax.ShapeDtypeStruct((MSG_ROWS, 12...  7.13 us
    pallas_call x1, Pallas kernels, receive(): pl.pallas_call(receive_kernel, out_shape=jax.ShapeDtypeStruct((ROWS, NLON...  5.18 us
    ppermute x1, starting transfers between devices, per_device(): south = lax.ppermute(field[:LEVS], 'lat', backward)  5.15 us
    pallas_call x1, Pallas kernels, stencil(): pl.pallas_call(stencil_kernel, out_shape=(jax.ShapeDtypeStruct((2, ROWS,...  3.32 us
  transfers between devices with their start and end apart: 2, of which 0 were waited for; matrix products, arithmetic and copies ran while one was open for 0% of the time, Pallas kernels for 2%

profile of v2, /device:TPU:1, one launch (start us, length us, event | category | flops | bytes accessed | tf_op | source)
XLA Modules:
  0.0 147.6 jit_solution(7150436438597113358)
XLA Ops:
  0.0 0.0 copy-start.4
  0.0 0.0 copy-start.2
  0.0 0.0 copy-start.5
  0.0 1.0 slice_bitcast_fusion
  1.0 5.1 %collective-permute-start.1 = (bf16[16,2560]{1,0:T(8,128)(2,1)S(1)}, bf16[16,2560]{1,0:T(8,128)(2,1)S(1)}, u32[]{:S(2)}, u32[]{:S(2)}) collective-permute-start(bf16[16,2560]{1,0:T(8,128)(2,1)S(1)} %get-tuple-element.13), channel_id=1, source_target_pairs={{4,0},{8,4},{12,8},{16,12},{20,16},{24,20},{28,24},{32,28},{36,32}... | collective-permute-start | bytes 245768 | tf_op jit(solution)/shard_map/ppermute | solution.py:381
  6.1 1.9 %collective-permute-start = (bf16[16,2560]{1,0:T(8,128)(2,1)S(1)}, bf16[16,2560]{1,0:T(8,128)(2,1)S(1)}, u32[]{:S(2)}, u32[]{:S(2)}) collective-permute-start(bf16[16,2560]{1,0:T(8,128)(2,1)S(1)} %get-tuple-element.14), channel_id=1, source_target_pairs={{0,4},{4,8},{8,12},{12,16},{16,20},{20,24},{24,28},{28,32},{32,36}... | collective-permute-start | bytes 245768 | tf_op jit(solution)/shard_map/ppermute | solution.py:380
  8.1 0.0 copy-start.1
  8.1 1.4 copy-done.1
  9.5 0.0 copy-start.3
  9.5 0.7 copy-done.3
  10.2 3.3 %stencil.1 = (bf16[2,320,1280]{2,1,0:T(8,128)(2,1)S(1)}, f32[2,2,16,1280]{3,2,1,0:T(8,128)S(1)}) custom-call(f32[3,20]{1,0:T(4,128)S(1)} %copy-done.3, bf16[320,2560]{1,0:T(8,128)(2,1)S(1)} %bitcast.21), custom_call_target="tpu_custom_call" | custom-call | flops 20000000 | bytes 4000000 | tf_op jit(solution)/shard_map/stencil/pallas_call | solution.py:113
  13.5 0.0 collective-permute-done.1.south_ref
  13.5 0.0 collective-permute-done.north_ref
  13.5 0.0 copy-done.4
  13.5 0.0 copy-done.2
  13.6 0.0 copy-done.5
  13.6 0.0 copy-start
  13.6 7.1 %send.1 = (bf16[6656,128]{1,0:T(8,128)(2,1)S(1)}, bf16[256,256]{1,0:T(8,128)(2,1)S(1)}) custom-call(f32[3,20]{1,0:T(4,128)S(1)} %copy-done.4, f32[1280]{0:T(1024)S(1)} %copy-done.5, s32[5,256]{1,0:T(8,128)S(1)} %bitcast.23, bf16[2,320,1280]{2,1,0:T(8,128)(2,1)S(1)} %get-tuple-element.9.part_ref, f32[2,2,16,1280]{3,2,1,0:T(8,128)S(1)} %get-tuple-element.10.edges_ref, ...), custom_call_target="tpu_custom_call" | custom-call | flops 2500000000 | bytes 12000000 | tf_op jit(solution)/shard_map/send/pallas_call | solution.py:191
  20.7 0.0 slice-start
  20.7 60.7 %all_to_all.10 = bf16[256,13,2,128]{3,2,1,0:T(2,128)(2,1)S(1)} all-to-all(bf16[256,13,2,128]{3,2,1,0:T(2,128)(2,1)S(1)} %bitcast.22), channel_id=1, replica_groups=mesh['lat'=64,'lev'=4] {'lev','lat'}, dimensions={0} | all-to-all | bytes 3407872 | tf_op jit(solution)/shard_map/all_to_all | solution.py:373
  81.4 0.0 copy-done
  81.4 0.0 slice-start.1
  81.4 10.2 %spectral.1 = bf16[6656,128]{1,0:T(8,128)(2,1)S(1)} custom-call(s32[5,256]{1,0:T(8,128)S(1)} %bitcast.24, bf16[6656,128]{1,0:T(8,128)(2,1)S(1)} %bitcast.16, bf16[1,3330,1280]{2,1,0:T(8,128)(2,1)S(1)} %copy-done), custom_call_target="tpu_custom_call" | custom-call | flops 2500000000 | bytes 12000000 | tf_op jit(solution)/shard_map/spectral/pallas_call | solution.py:298
  91.6 50.8 %all_to_all.11 = bf16[256,13,2,128]{3,2,1,0:T(2,128)(2,1)S(1)} all-to-all(bf16[256,13,2,128]{3,2,1,0:T(2,128)(2,1)S(1)} %bitcast.17), channel_id=1, replica_groups=mesh['lat'=64,'lev'=4] {'lev','lat'}, dimensions={0} | all-to-all | bytes 3407872 | tf_op jit(solution)/shard_map/all_to_all | solution.py:373
  142.4 0.0 slice-done
  142.4 0.0 slice-done.1
  142.4 5.2 %receive.1 = bf16[320,2560]{1,0:T(8,128)(2,1)} custom-call(bf16[6656,128]{1,0:T(8,128)(2,1)S(1)} %bitcast.15, bf16[256,256]{1,0:T(8,128)(2,1)S(1)} %get-tuple-element.12.pick_ref, bf16[5,2,1280,256]{3,2,1,0:T(8,128)(2,1)S(1)} %bitcast.19), custom_call_target="tpu_custom_call" | custom-call | flops 2500000000 | bytes 12000000 | tf_op jit(solution)/shard_map/receive/pallas_call | solution.py:351
  (1 shorter events, 0.0 us)
Async XLA Ops:
  0.0 13.5 %copy-start.4 = (f32[3,20]{1,0:T(4,128)S(1)}, f32[3,20]{1,0:T(4,128)}, u32[]{:S(2)}) copy-start(f32[3,20]{1,0:T(4,128)} %metric_ref.3) | copy-start | bytes 724
  0.0 13.5 %copy-start.2 = (s32[256,5]{0,1:T(8,128)S(1)}, s32[256,5]{0,1:T(8,128)}, u32[]{:S(2)}) copy-start(s32[256,5]{0,1:T(8,128)} %param.10) | copy-start | bytes 15364
  0.0 13.6 %copy-start.5 = (f32[1280]{0:T(1024)S(1)}, f32[1280]{0:T(1024)}, u32[]{:S(2)}) copy-start(f32[1280]{0:T(1024)} %quad_ref.1) | copy-start | bytes 15364
  1.0 12.5 %collective-permute-start.1 = (bf16[16,2560]{1,0:T(8,128)(2,1)S(1)}, bf16[16,2560]{1,0:T(8,128)(2,1)S(1)}, u32[]{:S(2)}, u32[]{:S(2)}) collective-permute-start(bf16[16,2560]{1,0:T(8,128)(2,1)S(1)} %get-tuple-element.13), channel_id=1, source_target_pairs={{4,0},{8,4},{12,8},{16,12},{20,16},{24,20},{28,24},{32,28},{36,32}... | collective-permute-start | bytes 245768 | tf_op jit(solution)/shard_map/ppermute | solution.py:381
  6.1 7.4 %collective-permute-start = (bf16[16,2560]{1,0:T(8,128)(2,1)S(1)}, bf16[16,2560]{1,0:T(8,128)(2,1)S(1)}, u32[]{:S(2)}, u32[]{:S(2)}) collective-permute-start(bf16[16,2560]{1,0:T(8,128)(2,1)S(1)} %get-tuple-element.14), channel_id=1, source_target_pairs={{0,4},{4,8},{8,12},{12,16},{16,20},{20,24},{24,28},{28,32},{32,36}... | collective-permute-start | bytes 245768 | tf_op jit(solution)/shard_map/ppermute | solution.py:380
  8.1 1.4 copy-start.1
  9.5 0.7 copy-start.3
  13.6 67.9 %copy-start = (bf16[1,3330,1280]{2,1,0:T(8,128)(2,1)S(1)}, bf16[1,3330,1280]{2,1,0:T(8,128)(2,1)}, u32[]{:S(2)}) copy-start(bf16[1,3330,1280]{2,1,0:T(8,128)(2,1)} %legendre_ref.1) | copy-start | bytes 25574404
  20.7 121.7 %slice-start = ((s8[6553600]{0:T(1024)(128)(4,1)}), s8[4194304]{0:T(1024)(128)(4,1)S(1)}, s32[]{:S(2)}) async-start(s8[6553600]{0:T(1024)(128)(4,1)} %bitcast.18), calls=%async_computation.2 | async-start | bytes 8388608
  81.4 61.0 %slice-start.1 = ((s8[6553600]{0:T(1024)(128)(4,1)}), s8[2359296]{0:T(1024)(128)(4,1)S(1)}, s32[]{:S(2)}) async-start(s8[6553600]{0:T(1024)(128)(4,1)} %bitcast.18), calls=%async_computation.3 | async-start | bytes 4718592

commit v3 on v2

--- a/solution.py
+++ b/solution.py
@@ -23,7 +23,7 @@
 CAP = 3330
 VMEM_LIMIT = 32 * 1024 * 1024
 SEND_LIMIT = 48 * 1024 * 1024
-STENCIL_LIMIT = 16 * 1024 * 1024
+LOAD_LIMIT = 57 * 1024 * 1024
 AXES = ("lev", "lat")
 
 
@@ -84,48 +84,41 @@
         target[where, :] = source[where, :].astype(target.dtype)
 
 
-def stencil_kernel(metric_ref, field_ref, halves_ref, edges_ref):
-    def band(lat):
-        return field_ref[pl.ds(pl.multiple_of(lat * LEVS, LEVS), LEVS), :].astype(jnp.float32)
-
-    def stencil(lat, north, south):
-        centre = band(lat)
-        zonal = pltpu.roll(centre, 1, 1) + pltpu.roll(centre, NLON - 1, 1) - 2.0 * centre
-        toward = -centre if north is None else north - centre
-        away = -centre if south is None else south - centre
-        total = metric_ref[0, lat] * toward + metric_ref[1, lat] * away
-        total = total + metric_ref[2, lat] * zonal
-        return total[:, :HALF] + total[:, HALF:], total[:, :HALF] - total[:, HALF:]
-
-    edges_ref[0, 0], edges_ref[0, 1] = stencil(0, None, band(1))
-    edges_ref[1, 0], edges_ref[1, 1] = stencil(BAND - 1, band(BAND - 2), None)
-
-    @pl.loop(1, BAND - 1)
-    def _(lat):
-        both = stencil(lat, band(lat - 1), band(lat + 1))
-        where = pl.ds(pl.multiple_of(lat * LEVS, LEVS), LEVS)
-        halves_ref[0, where, :] = both[0].astype(jnp.bfloat16)
-        halves_ref[1, where, :] = both[1].astype(jnp.bfloat16)
-
-
-def stencil(metric, field):
-    vmem = pl.BlockSpec(memory_space=pltpu.VMEM)
+def load_kernel(field_ref, metric_ref, quad_ref, sets_ref, *refs):
+    first_ref, last_ref, field_out, metric_out, quad_out, sets_out, landed = refs
+    moves = [
+        (field_ref.at[pl.ds(0, LEVS)], first_ref),
+        (field_ref.at[pl.ds(ROWS - LEVS, LEVS)], last_ref),
+        (field_ref, field_out),
+        (metric_ref, metric_out),
+        (quad_ref, quad_out),
+        (sets_ref, sets_out),
+    ]
+    copies = [pltpu.make_async_copy(here, there, landed.at[i]) for i, (here, there) in enumerate(moves)]
+    for copy in copies:
+        copy.start()
+    for copy in copies:
+        copy.wait()
+
+
+def load(*arrays):
+    field = arrays[0]
+    halo = (LEVS, NLON)
+    shapes = [(halo, field.dtype), (halo, field.dtype)] + [(a.shape, a.dtype) for a in arrays]
     return pl.pallas_call(
-        stencil_kernel,
-        out_shape=(
-            jax.ShapeDtypeStruct((2, ROWS, HALF), jnp.bfloat16),
-            jax.ShapeDtypeStruct((2, 2, LEVS, HALF), jnp.float32),
-        ),
-        in_specs=[pl.BlockSpec(memory_space=pltpu.SMEM), vmem],
-        out_specs=(vmem, vmem),
-        compiler_params=pltpu.CompilerParams(vmem_limit_bytes=STENCIL_LIMIT),
-        cost_estimate=pl.CostEstimate(flops=20_000_000, bytes_accessed=4_000_000, transcendentals=0),
-        name="stencil",
-    )(metric, field)
+        load_kernel,
+        out_shape=tuple(pltpu.VMEM(*shape) for shape in shapes),
+        in_specs=[pl.BlockSpec(memory_space=pl.ANY)] * len(arrays),
+        out_specs=tuple([pl.BlockSpec(memory_space=pltpu.VMEM)] * len(shapes)),
+        scratch_shapes=[pltpu.SemaphoreType.DMA((len(shapes),))],
+        compiler_params=pltpu.CompilerParams(vmem_limit_bytes=LOAD_LIMIT),
+        cost_estimate=pl.CostEstimate(flops=0, bytes_accessed=4_000_000, transcendentals=0),
+        name="load",
+    )(*arrays)
 
 
 def send_kernel(
-    metric_ref, quad_ref, sets_ref, part_ref, edges_ref, north_ref, south_ref, table_ref,
+    metric_ref, quad_ref, sets_ref, field_ref, north_ref, south_ref, table_ref,
     out_ref, pick_ref, halves, mixed, rows, picks, tables, landed,
 ):
     slot = pl.program_id(0)
@@ -137,14 +130,26 @@
     def _():
         for which in range(SLOTS):
             fetch(which).start()
-        for edge, (lat, halo) in enumerate(((0, north_ref), (BAND - 1, south_ref))):
-            value = halo[...].astype(jnp.float32) * metric_ref[edge, lat]
-            first, second = value[:, :HALF], value[:, HALF:]
-            where = slice(lat * LEVS, (lat + 1) * LEVS)
-            halves[0, where, :] = (edges_ref[edge, 0] + (first + second)).astype(jnp.bfloat16)
-            halves[1, where, :] = (edges_ref[edge, 1] + (first - second)).astype(jnp.bfloat16)
-        inner = slice(LEVS, ROWS - LEVS)
-        halves[:, inner, :] = part_ref[:, inner, :]
+
+        def band(lat):
+            return field_ref[pl.ds(pl.multiple_of(lat * LEVS, LEVS), LEVS), :].astype(jnp.float32)
+
+        def stencil(lat, north, south):
+            centre = band(lat)
+            zonal = pltpu.roll(centre, 1, 1) + pltpu.roll(centre, NLON - 1, 1) - 2.0 * centre
+            total = metric_ref[0, lat] * (north - centre) + metric_ref[1, lat] * (south - centre)
+            total = total + metric_ref[2, lat] * zonal
+            first, second = total[:, :HALF], total[:, HALF:]
+            where = pl.ds(pl.multiple_of(lat * LEVS, LEVS), LEVS)
+            halves[0, where, :] = (first + second).astype(jnp.bfloat16)
+            halves[1, where, :] = (first - second).astype(jnp.bfloat16)
+
+        stencil(0, north_ref[...].astype(jnp.float32), band(1))
+        stencil(BAND - 1, band(BAND - 2), south_ref[...].astype(jnp.float32))
+
+        @pl.loop(1, BAND - 1)
+        def _(lat):
+            stencil(lat, band(lat - 1), band(lat + 1))
 
         sets = sets_ref[0:1, :]
         position = (sets % 2) * (SETS // 2) + sets // 2
@@ -182,7 +187,7 @@
         copy_rows(out_ref, rows)
 
 
-def send(metric, quad, sets, part, edges, north, south, table):
+def send(metric, quad, sets, field, north, south, table):
     smem = pl.BlockSpec(memory_space=pltpu.SMEM)
 
     def whole(*shape):
@@ -199,8 +204,7 @@
             smem,
             smem,
             whole(SLOTS, SETS),
-            whole(2, ROWS, HALF),
-            whole(2, 2, LEVS, HALF),
+            whole(ROWS, NLON),
             whole(LEVS, NLON),
             whole(LEVS, NLON),
             pl.BlockSpec(memory_space=pltpu.HBM),
@@ -217,13 +221,15 @@
         compiler_params=pltpu.CompilerParams(vmem_limit_bytes=SEND_LIMIT),
         cost_estimate=pl.CostEstimate(flops=2_500_000_000, bytes_accessed=12_000_000, transcendentals=0),
         name="send",
-    )(metric, quad, sets, part, edges, north, south, table)
+    )(metric, quad, sets, field, north, south, table)
 
 
 BLOCKS = [(0, 1), (0, 1), (0, 1), (0, 1), (0, 2), (1, 1), (1, 1), (1, 1), (1, 2), (2, 1), (2, 2), (2, 2), (3, 2)]
 
 
-def spectral_kernel(sets_ref, got_ref, legendre_ref, out_ref, rows, column, weighted, reduced, tail):
+def spectral_kernel(
+    sets_ref, got_ref, legendre_ref, out_ref, rows, rows_back, columns, weighted, reduced, tail
+):
     number = sets_ref[0, lax.axis_index("lat") * LEV_DEVS + lax.axis_index("lev")]
     starts = (0, NLAT - number, 2049, 2817 - number, 3074, CAP - number)
     bases = (number, -769, number - 1537, -1794, number - 2050)
@@ -238,18 +244,21 @@
                 for lev in range(LEV_DEVS)
             ]
             for group, tile in enumerate(block_exchange(tiles)):
-                column[pl.ds(4 * part + group, LAT_DEVS, stride=BAND), :] = tile
-        weighted[:, slot * 128 : slot * 128 + 128] = column[...].astype(jnp.bfloat16)
+                columns[pl.ds(slot * NLAT + 4 * part + group, LAT_DEVS, stride=BAND), :] = tile
+        weighted[:, slot * 128 : slot * 128 + 128] = columns[
+            slot * NLAT : slot * NLAT + NLAT, :
+        ].astype(jnp.bfloat16)
 
     def damp(coeffs, first_row, slots):
-        ids = lax.broadcasted_iota(jnp.int32, (coeffs.shape[0], 128), 0) + first_row
+        ids = lax.broadcasted_iota(jnp.int32, (1, coeffs.shape[0]), 1) + first_row
         pieces = []
         for place, slot in enumerate(slots):
             degree = (ids + bases[slot]).astype(jnp.float32)
             valid = (ids >= starts[slot]) & (ids < starts[slot + 1])
             bottom = 1.0 + degree * (degree + 1.0) * (4.0 / float(NLAT * NLAT))
-            part = coeffs[:, place * 128 : place * 128 + 128]
-            pieces.append(jnp.where(valid, part / bottom, 0.0))
+            factor = jnp.where(valid, 1.0 / bottom, 0.0)
+            part = coeffs[:, place * 128 : place * 128 + 128].T
+            pieces.append((part * factor).astype(jnp.bfloat16))
         return pieces
 
     spans = [[None, 0] for _ in range(SLOTS)]
@@ -265,13 +274,12 @@
                 spans[slot][0] = block
             place = (block - spans[slot][0]) * 256
             spans[slot][1] = place + 256
-            reduced[slot, :, place : place + 256] = piece.T.astype(jnp.bfloat16)
+            reduced[slot, :, place : place + 256] = piece
     tail[...] = jnp.zeros_like(tail)
     tail[0:2, :] = legendre_ref[0, 3328:3330, :]
     coeffs = jnp.dot(tail[...], weighted[:, 512:640], preferred_element_type=jnp.float32)
-    last = jnp.concatenate(
-        [damp(coeffs, 3328, (4,))[0], jnp.zeros((112, 128), jnp.float32)], axis=0
-    ).T.astype(jnp.bfloat16)[:, :16]
+    coeffs = jnp.concatenate([coeffs, jnp.zeros((112, 128), jnp.float32)], axis=0)
+    last = damp(coeffs, 3328, (4,))[0][:, :16]
 
     for slot in range(SLOTS):
         first, length = spans[slot]
@@ -282,16 +290,17 @@
         )
         if slot == SLOTS - 1:
             back = back + jnp.dot(last, tail[...], preferred_element_type=jnp.float32)
-        column[...] = back.T
+        columns[slot * NLAT : slot * NLAT + NLAT, :] = back.T
         for part in range(5):
             tiles = [
-                column[pl.ds(4 * part + group, LAT_DEVS, stride=BAND), :] for group in range(4)
+                columns[pl.ds(slot * NLAT + 4 * part + group, LAT_DEVS, stride=BAND), :]
+                for group in range(4)
             ]
             row = slot * 5 + part
             for lev, tile in enumerate(block_exchange(tiles)):
-                rows[pl.ds(lev * LAT_DEVS * PITCH + row, LAT_DEVS, stride=PITCH), :] = tile
-
-    copy_rows(out_ref, rows)
+                rows_back[pl.ds(lev * LAT_DEVS * PITCH + row, LAT_DEVS, stride=PITCH), :] = tile
+
+    copy_rows(out_ref, rows_back)
 
 
 def spectral(sets, got, legendre):
@@ -306,7 +315,8 @@
         out_specs=pl.BlockSpec(memory_space=pltpu.VMEM),
         scratch_shapes=[
             pltpu.VMEM((MSG_ROWS, 128), jnp.float32),
-            pltpu.VMEM((NLAT, 128), jnp.float32),
+            pltpu.VMEM((MSG_ROWS, 128), jnp.float32),
+            pltpu.VMEM((SLOTS * NLAT, 128), jnp.float32),
             pltpu.VMEM((NLAT, SLOTS * 128), jnp.bfloat16),
             pltpu.VMEM((SLOTS, 128, NLAT), jnp.bfloat16),
             pltpu.VMEM((16, NLAT), jnp.bfloat16),
@@ -377,11 +387,10 @@
     field = jnp.transpose(field, (1, 0, 2)).reshape(ROWS, NLON)
     forward = [(i, i + 1) for i in range(LAT_DEVS - 1)]
     backward = [(i + 1, i) for i in range(LAT_DEVS - 1)]
-    north = lax.ppermute(field[ROWS - LEVS :], "lat", forward)
-    south = lax.ppermute(field[:LEVS], "lat", backward)
-    part, edges = stencil(metric, field)
-    sets = assignment.T
-    message, pick = send(metric, quad_weight, sets, part, edges, north, south, forward_table())
+    first, last, field, metric, quad, sets = load(field, metric, quad_weight, assignment.T)
+    north = lax.ppermute(last, "lat", forward)
+    south = lax.ppermute(first, "lat", backward)
+    message, pick = send(metric, quad, sets, field, north, south, forward_table())
     back = exchange(spectral(sets, exchange(message), legendre))
     out = receive(back, pick, inverse_table())
     return jnp.transpose(out.reshape(BAND, LEVS, NLON), (1, 0, 2))

time: 148 us -> 147 us (level)
  waiting for transfers between devices: 0.01 us -> 3.82 us
  local copies, waits for them, and re-layouts: 3.11 us -> 0.01 us
    ppermute x2, waiting for transfers between devices: 0.01 us -> 3.82 us  [the longest x1 3.82 us: per_device(): south = lax.ppermute(first, 'lat', backward)]
    unnamed x16 -> x6, local copies, waits for them, and re-layouts: 2.13 us -> 0.01 us
    pallas_call x1, Pallas kernels: 3.32 us -> 1.58 us  [load(): pl.pallas_call(load_kernel, out_shape=tuple((pltpu.VMEM(*shape) for shape...]
  transfers between devices with their start and end apart: 2 -> 2, of which waited for: 0 -> 1; matrix products, arithmetic and copies ran while one was open for 0% -> 0% of each run, Pallas kernels for 2% -> 0%
where the time goes in v3:
time: 147 us
  blocking collectives  111 us (76%)
  Pallas kernels  25.3 us (17%)
  starting transfers between devices  6.86 us (5%)
  waiting for transfers between devices  3.82 us (3%)
    all_to_all x2, blocking collectives, exchange(): lax.all_to_all(pairs, AXES, split_axis=0, concat_axis=0, tiled=True)  111 us
    pallas_call x1, Pallas kernels, spectral(): pl.pallas_call(spectral_kernel, out_shape=jax.ShapeDtypeStruct((MSG_ROWS,...  10.1 us
    pallas_call x1, Pallas kernels, send(): pl.pallas_call(send_kernel, out_shape=(jax.ShapeDtypeStruct((MSG_ROWS, 12...  8.44 us
    pallas_call x1, Pallas kernels, receive(): pl.pallas_call(receive_kernel, out_shape=jax.ShapeDtypeStruct((ROWS, NLON...  5.18 us
    ppermute x1, starting transfers between devices, per_device(): north = lax.ppermute(last, 'lat', forward)  4.94 us
    ppermute x1, waiting for transfers between devices, per_device(): south = lax.ppermute(first, 'lat', backward)  3.82 us
  transfers between devices with their start and end apart: 2, of which 1 were waited for; matrix products, arithmetic and copies ran while one was open for 0% of the time, Pallas kernels for 0%

profile of v3, /device:TPU:1, one launch (start us, length us, event | category | flops | bytes accessed | tf_op | source)
XLA Modules:
  0.0 147.3 jit_solution(3092521406682691755)
XLA Ops:
  0.0 1.6 %load.1 = (bf16[16,2560]{1,0:T(8,128)(2,1)S(1)}, bf16[16,2560]{1,0:T(8,128)(2,1)S(1)}, bf16[320,2560]{1,0:T(8,128)(2,1)S(1)}, f32[3,20]{1,0:T(4,128)S(1)}, f32[1280]{0:T(1024)S(1)}, /*index=5*/s32[5,256]{1,0:T(8,128)S(1)}) custom-call(bf16[320,2560]{1,0:T(8,128)(2,1)} %bitcast.17, f32[3,20]{1,0:T(4,128)} %metric_ref.1, f32[1280]{0:T(1024)} %quad_ref.1, ...), custom_call_target="tpu_custom_call" | custom-call | bytes 4000000 | tf_op jit(solution)/shard_map/load/pallas_call | solution.py:108
  1.6 4.9 %collective-permute-start = (bf16[16,2560]{1,0:T(8,128)(2,1)S(1)}, bf16[16,2560]{1,0:T(8,128)(2,1)S(1)}, u32[]{:S(2)}, u32[]{:S(2)}) collective-permute-start(bf16[16,2560]{1,0:T(8,128)(2,1)S(1)} %get-tuple-element.17), channel_id=1, source_target_pairs={{0,4},{4,8},{8,12},{12,16},{16,20},{20,24},{24,28},{28,32},{32,36}... | collective-permute-start | bytes 245768 | tf_op jit(solution)/shard_map/ppermute | solution.py:391
  6.5 1.9 %collective-permute-start.1 = (bf16[16,2560]{1,0:T(8,128)(2,1)S(1)}, bf16[16,2560]{1,0:T(8,128)(2,1)S(1)}, u32[]{:S(2)}, u32[]{:S(2)}) collective-permute-start(bf16[16,2560]{1,0:T(8,128)(2,1)S(1)} %get-tuple-element.18), channel_id=1, source_target_pairs={{4,0},{8,4},{12,8},{16,12},{20,16},{24,20},{28,24},{32,28},{36,32}... | collective-permute-start | bytes 245768 | tf_op jit(solution)/shard_map/ppermute | solution.py:392
  8.5 0.0 collective-permute-done.north_ref
  8.5 3.8 %collective-permute-done.1.south_ref = bf16[16,2560]{1,0:T(8,128)(2,1)S(1)} collective-permute-done((bf16[16,2560]{1,0:T(8,128)(2,1)S(1)}, bf16[16,2560]{1,0:T(8,128)(2,1)S(1)}, u32[]{:S(2)}, u32[]{:S(2)}) %collective-permute-start.1) | collective-permute-done | bytes 81952 | tf_op jit(solution)/shard_map/ppermute | solution.py:392
  12.3 0.0 copy-start
  12.3 8.4 %send.1 = (bf16[6656,128]{1,0:T(8,128)(2,1)S(1)}, bf16[256,256]{1,0:T(8,128)(2,1)S(1)}) custom-call(f32[3,20]{1,0:T(4,128)S(1)} %get-tuple-element.14.metric_ref, f32[1280]{0:T(1024)S(1)} %get-tuple-element.15.quad_ref, s32[5,256]{1,0:T(8,128)S(1)} %get-tuple-element.13.sets_ref, bf16[320,2560]{1,0:T(8,128)(2,1)S(1)} %get-tuple-element.16.field_ref, ...), custom_call_target="tpu_custom_call" | custom-call | flops 2500000000 | bytes 12000000 | tf_op jit(solution)/shard_map/send/pallas_call | solution.py:196
  20.8 0.0 slice-start
  20.8 60.4 %all_to_all.10 = bf16[256,13,2,128]{3,2,1,0:T(2,128)(2,1)S(1)} all-to-all(bf16[256,13,2,128]{3,2,1,0:T(2,128)(2,1)S(1)} %bitcast.16), channel_id=1, replica_groups=mesh['lat'=64,'lev'=4] {'lev','lat'}, dimensions={0} | all-to-all | bytes 3407872 | tf_op jit(solution)/shard_map/all_to_all | solution.py:383
  81.2 0.0 copy-done
  81.2 0.0 slice-start.1
  81.2 10.1 %spectral.1 = bf16[6656,128]{1,0:T(8,128)(2,1)S(1)} custom-call(s32[5,256]{1,0:T(8,128)S(1)} %get-tuple-element.13.sets_ref, bf16[6656,128]{1,0:T(8,128)(2,1)S(1)} %bitcast.12, bf16[1,3330,1280]{2,1,0:T(8,128)(2,1)S(1)} %copy-done), custom_call_target="tpu_custom_call" | custom-call | flops 2500000000 | bytes 12000000 | tf_op jit(solution)/shard_map/spectral/pallas_call | solution.py:307
  91.3 50.8 %all_to_all.11 = bf16[256,13,2,128]{3,2,1,0:T(2,128)(2,1)S(1)} all-to-all(bf16[256,13,2,128]{3,2,1,0:T(2,128)(2,1)S(1)} %bitcast.13), channel_id=1, replica_groups=mesh['lat'=64,'lev'=4] {'lev','lat'}, dimensions={0} | all-to-all | bytes 3407872 | tf_op jit(solution)/shard_map/all_to_all | solution.py:383
  142.1 0.0 slice-done
  142.1 0.0 slice-done.1
  142.1 5.2 %receive.1 = bf16[320,2560]{1,0:T(8,128)(2,1)} custom-call(bf16[6656,128]{1,0:T(8,128)(2,1)S(1)} %bitcast.11, bf16[256,256]{1,0:T(8,128)(2,1)S(1)} %get-tuple-element.20.pick_ref, bf16[5,2,1280,256]{3,2,1,0:T(8,128)(2,1)S(1)} %bitcast.15), custom_call_target="tpu_custom_call" | custom-call | flops 2500000000 | bytes 12000000 | tf_op jit(solution)/shard_map/receive/pallas_call | solution.py:361
  (1 shorter events, 0.0 us)
Async XLA Ops:
  1.6 6.9 %collective-permute-start = (bf16[16,2560]{1,0:T(8,128)(2,1)S(1)}, bf16[16,2560]{1,0:T(8,128)(2,1)S(1)}, u32[]{:S(2)}, u32[]{:S(2)}) collective-permute-start(bf16[16,2560]{1,0:T(8,128)(2,1)S(1)} %get-tuple-element.17), channel_id=1, source_target_pairs={{0,4},{4,8},{8,12},{12,16},{16,20},{20,24},{24,28},{28,32},{32,36}... | collective-permute-start | bytes 245768 | tf_op jit(solution)/shard_map/ppermute | solution.py:391
  6.5 5.8 %collective-permute-start.1 = (bf16[16,2560]{1,0:T(8,128)(2,1)S(1)}, bf16[16,2560]{1,0:T(8,128)(2,1)S(1)}, u32[]{:S(2)}, u32[]{:S(2)}) collective-permute-start(bf16[16,2560]{1,0:T(8,128)(2,1)S(1)} %get-tuple-element.18), channel_id=1, source_target_pairs={{4,0},{8,4},{12,8},{16,12},{20,16},{24,20},{28,24},{32,28},{36,32}... | collective-permute-start | bytes 245768 | tf_op jit(solution)/shard_map/ppermute | solution.py:392
  12.3 68.9 %copy-start = (bf16[1,3330,1280]{2,1,0:T(8,128)(2,1)S(1)}, bf16[1,3330,1280]{2,1,0:T(8,128)(2,1)}, u32[]{:S(2)}) copy-start(bf16[1,3330,1280]{2,1,0:T(8,128)(2,1)} %legendre_ref.1) | copy-start | bytes 25574404
  20.8 121.3 %slice-start = ((s8[6553600]{0:T(1024)(128)(4,1)}), s8[4194304]{0:T(1024)(128)(4,1)S(1)}, s32[]{:S(2)}) async-start(s8[6553600]{0:T(1024)(128)(4,1)} %bitcast.14), calls=%async_computation.2 | async-start | bytes 8388608
  81.2 60.9 %slice-start.1 = ((s8[6553600]{0:T(1024)(128)(4,1)}), s8[2359296]{0:T(1024)(128)(4,1)S(1)}, s32[]{:S(2)}) async-start(s8[6553600]{0:T(1024)(128)(4,1)} %bitcast.14), calls=%async_computation.3 | async-start | bytes 4718592

commit v4 on v3

--- a/solution.py
+++ b/solution.py
@@ -60,21 +60,17 @@
     return np.ascontiguousarray(table).astype(jnp.bfloat16)
 
 
-def block_exchange(tiles):
+def rotated(tile, groups):
+    shift = 32 * groups % 128
+    return pltpu.roll(tile, shift, 1) if shift else tile
+
+
+def regrouped(tiles):
     lanes = lax.broadcasted_iota(jnp.int32, tiles[0].shape, 1)
     low = lanes < 64
     even = (lanes // 32) % 2 == 0
-    mixed = [None] * 4
-    for one in (0, 1):
-        first, second = tiles[one], tiles[one + 2]
-        mixed[one] = jnp.where(low, first, pltpu.roll(second, 64, 1))
-        mixed[one + 2] = jnp.where(low, pltpu.roll(first, 64, 1), second)
-    done = [None] * 4
-    for one in (0, 2):
-        first, second = mixed[one], mixed[one + 1]
-        done[one] = jnp.where(even, first, pltpu.roll(second, 32, 1))
-        done[one + 1] = jnp.where(even, pltpu.roll(first, 96, 1), second)
-    return done
+    pairs = [jnp.where(even, tiles[i], tiles[(i + 1) % 4]) for i in range(4)]
+    return [jnp.where(low, pairs[-i % 4], pairs[(2 - i) % 4]) for i in range(4)]
 
 
 def copy_rows(target, source):
@@ -163,6 +159,7 @@
                 ].astype(jnp.bfloat16)
 
     first_lat = lax.axis_index("lat") * BAND
+    lev_index = lax.axis_index("lev")
     fetch(slot).wait()
     for odd in range(2):
         waves = jnp.dot(
@@ -171,9 +168,10 @@
         for lat in range(BAND):
             weight = quad_ref[first_lat + lat]
             weighted = (waves[lat * LEVS : (lat + 1) * LEVS] * weight).astype(jnp.bfloat16)
+            place = 4 * (lat // 4) + (lat + lev_index) % 4
             for part in range(2):
-                start = (2 * lat + part) * LEVS
-                mixed[start : start + LEVS, odd * 128 : odd * 128 + 128] = weighted[
+                start = pl.multiple_of((2 * place + part) * LEVS, LEVS)
+                mixed[pl.ds(start, LEVS), odd * 128 : odd * 128 + 128] = weighted[
                     :, part * 128 : part * 128 + 128
                 ]
     dealt = lax.dot_general(
@@ -243,8 +241,9 @@
                 rows[pl.ds(lev * LAT_DEVS * PITCH + row, LAT_DEVS, stride=PITCH), :]
                 for lev in range(LEV_DEVS)
             ]
-            for group, tile in enumerate(block_exchange(tiles)):
-                columns[pl.ds(slot * NLAT + 4 * part + group, LAT_DEVS, stride=BAND), :] = tile
+            for group, tile in enumerate(regrouped(tiles)):
+                where = pl.ds(slot * NLAT + 4 * part + group, LAT_DEVS, stride=BAND)
+                columns[where, :] = rotated(tile, -group)
         weighted[:, slot * 128 : slot * 128 + 128] = columns[
             slot * NLAT : slot * NLAT + NLAT, :
         ].astype(jnp.bfloat16)
@@ -293,11 +292,11 @@
         columns[slot * NLAT : slot * NLAT + NLAT, :] = back.T
         for part in range(5):
             tiles = [
-                columns[pl.ds(slot * NLAT + 4 * part + group, LAT_DEVS, stride=BAND), :]
+                rotated(columns[pl.ds(slot * NLAT + 4 * part + group, LAT_DEVS, stride=BAND), :], group)
                 for group in range(4)
             ]
             row = slot * 5 + part
-            for lev, tile in enumerate(block_exchange(tiles)):
+            for lev, tile in enumerate(regrouped(tiles)):
                 rows_back[pl.ds(lev * LAT_DEVS * PITCH + row, LAT_DEVS, stride=PITCH), :] = tile
 
     copy_rows(out_ref, rows_back)
@@ -329,6 +328,7 @@
 
 def receive_kernel(got_ref, pick_ref, table_ref, out_ref, rows, waves):
     block = pl.program_id(0)
+    lev_index = lax.axis_index("lev")
 
     @pl.when(block == 0)
     def _():
@@ -341,11 +341,12 @@
                     tile.T.astype(jnp.bfloat16), pick_ref[...], preferred_element_type=jnp.float32
                 ).astype(jnp.bfloat16)
                 for group in range(8):
-                    lat, side = 4 * part + group // 2, group % 2
+                    lat, side = 4 * part + (group // 2 + LEV_DEVS - lev_index) % 4, group % 2
+                    row = pl.multiple_of(lat * LEVS, LEVS)
                     for parity in range(2):
                         odd = (slot + parity) % 2
                         place = (2 * slot + side) * 128
-                        waves[parity, lat * LEVS : lat * LEVS + LEVS, place : place + 128] = dealt[
+                        waves[parity, pl.ds(row, LEVS), place : place + 128] = dealt[
                             group * LEVS : group * LEVS + LEVS, odd * 128 : odd * 128 + 128
                         ]
 

time: 147 us -> 145 us (0.986)
  Pallas kernels: 25.3 us -> 22.7 us
    pallas_call x1, Pallas kernels: 10.1 us -> 6.96 us  [spectral(): pl.pallas_call(spectral_kernel, out_shape=jax.ShapeDtypeStruct((MSG_ROWS,...]
where the time goes in v4:
time: 145 us
  blocking collectives  111 us (77%)
  Pallas kernels  22.7 us (16%)
  starting transfers between devices  6.86 us (5%)
  waiting for transfers between devices  3.82 us (3%)
    all_to_all x2, blocking collectives, exchange(): lax.all_to_all(pairs, AXES, split_axis=0, concat_axis=0, tiled=True)  111 us
    pallas_call x1, Pallas kernels, send(): pl.pallas_call(send_kernel, out_shape=(jax.ShapeDtypeStruct((MSG_ROWS, 12...  8.85 us
    pallas_call x1, Pallas kernels, spectral(): pl.pallas_call(spectral_kernel, out_shape=jax.ShapeDtypeStruct((MSG_ROWS,...  6.96 us
    pallas_call x1, Pallas kernels, receive(): pl.pallas_call(receive_kernel, out_shape=jax.ShapeDtypeStruct((ROWS, NLON...  5.27 us
    ppermute x1, starting transfers between devices, per_device(): north = lax.ppermute(last, 'lat', forward)  4.94 us
    ppermute x1, waiting for transfers between devices, per_device(): south = lax.ppermute(first, 'lat', backward)  3.82 us
  transfers between devices with their start and end apart: 2, of which 1 were waited for; matrix products, arithmetic and copies ran while one was open for 0% of the time, Pallas kernels for 0%

profile of v4, /device:TPU:1, one launch (start us, length us, event | category | flops | bytes accessed | tf_op | source)
XLA Modules:
  0.0 144.7 jit_solution(14182940813032529230)
XLA Ops:
  0.0 1.6 %load.1 = (bf16[16,2560]{1,0:T(8,128)(2,1)S(1)}, bf16[16,2560]{1,0:T(8,128)(2,1)S(1)}, bf16[320,2560]{1,0:T(8,128)(2,1)S(1)}, f32[3,20]{1,0:T(4,128)S(1)}, f32[1280]{0:T(1024)S(1)}, /*index=5*/s32[5,256]{1,0:T(8,128)S(1)}) custom-call(bf16[320,2560]{1,0:T(8,128)(2,1)} %bitcast.17, f32[3,20]{1,0:T(4,128)} %metric_ref.1, f32[1280]{0:T(1024)} %quad_ref.1, ...), custom_call_target="tpu_custom_call" | custom-call | bytes 4000000 | tf_op jit(solution)/shard_map/load/pallas_call | solution.py:104
  1.6 4.9 %collective-permute-start = (bf16[16,2560]{1,0:T(8,128)(2,1)S(1)}, bf16[16,2560]{1,0:T(8,128)(2,1)S(1)}, u32[]{:S(2)}, u32[]{:S(2)}) collective-permute-start(bf16[16,2560]{1,0:T(8,128)(2,1)S(1)} %get-tuple-element.17), channel_id=1, source_target_pairs={{0,4},{4,8},{8,12},{12,16},{16,20},{20,24},{24,28},{28,32},{32,36}... | collective-permute-start | bytes 245768 | tf_op jit(solution)/shard_map/ppermute | solution.py:392
  6.5 1.9 %collective-permute-start.1 = (bf16[16,2560]{1,0:T(8,128)(2,1)S(1)}, bf16[16,2560]{1,0:T(8,128)(2,1)S(1)}, u32[]{:S(2)}, u32[]{:S(2)}) collective-permute-start(bf16[16,2560]{1,0:T(8,128)(2,1)S(1)} %get-tuple-element.18), channel_id=1, source_target_pairs={{4,0},{8,4},{12,8},{16,12},{20,16},{24,20},{28,24},{32,28},{36,32}... | collective-permute-start | bytes 245768 | tf_op jit(solution)/shard_map/ppermute | solution.py:393
  8.5 0.0 collective-permute-done.north_ref
  8.5 3.8 %collective-permute-done.1.south_ref = bf16[16,2560]{1,0:T(8,128)(2,1)S(1)} collective-permute-done((bf16[16,2560]{1,0:T(8,128)(2,1)S(1)}, bf16[16,2560]{1,0:T(8,128)(2,1)S(1)}, u32[]{:S(2)}, u32[]{:S(2)}) %collective-permute-start.1) | collective-permute-done | bytes 81952 | tf_op jit(solution)/shard_map/ppermute | solution.py:393
  12.3 0.0 copy-start
  12.3 8.9 %send.1 = (bf16[6656,128]{1,0:T(8,128)(2,1)S(1)}, bf16[256,256]{1,0:T(8,128)(2,1)S(1)}) custom-call(f32[3,20]{1,0:T(4,128)S(1)} %get-tuple-element.14.metric_ref, f32[1280]{0:T(1024)S(1)} %get-tuple-element.15.quad_ref, s32[5,256]{1,0:T(8,128)S(1)} %get-tuple-element.13.sets_ref, bf16[320,2560]{1,0:T(8,128)(2,1)S(1)} %get-tuple-element.16.field_ref, ...), custom_call_target="tpu_custom_call" | custom-call | flops 2500000000 | bytes 12000000 | tf_op jit(solution)/shard_map/send/pallas_call | solution.py:194
  21.2 0.0 slice-start
  21.2 60.4 %all_to_all.10 = bf16[256,13,2,128]{3,2,1,0:T(2,128)(2,1)S(1)} all-to-all(bf16[256,13,2,128]{3,2,1,0:T(2,128)(2,1)S(1)} %bitcast.16), channel_id=1, replica_groups=mesh['lat'=64,'lev'=4] {'lev','lat'}, dimensions={0} | all-to-all | bytes 3407872 | tf_op jit(solution)/shard_map/all_to_all | solution.py:384
  81.6 0.0 copy-done
  81.6 0.0 slice-start.1
  81.6 7.0 %spectral.1 = bf16[6656,128]{1,0:T(8,128)(2,1)S(1)} custom-call(s32[5,256]{1,0:T(8,128)S(1)} %get-tuple-element.13.sets_ref, bf16[6656,128]{1,0:T(8,128)(2,1)S(1)} %bitcast.12, bf16[1,3330,1280]{2,1,0:T(8,128)(2,1)S(1)} %copy-done), custom_call_target="tpu_custom_call" | custom-call | flops 2500000000 | bytes 12000000 | tf_op jit(solution)/shard_map/spectral/pallas_call | solution.py:306
  88.6 50.8 %all_to_all.11 = bf16[256,13,2,128]{3,2,1,0:T(2,128)(2,1)S(1)} all-to-all(bf16[256,13,2,128]{3,2,1,0:T(2,128)(2,1)S(1)} %bitcast.13), channel_id=1, replica_groups=mesh['lat'=64,'lev'=4] {'lev','lat'}, dimensions={0} | all-to-all | bytes 3407872 | tf_op jit(solution)/shard_map/all_to_all | solution.py:384
  139.4 0.0 slice-done
  139.4 0.0 slice-done.1
  139.4 5.3 %receive.1 = bf16[320,2560]{1,0:T(8,128)(2,1)} custom-call(bf16[6656,128]{1,0:T(8,128)(2,1)S(1)} %bitcast.11, bf16[256,256]{1,0:T(8,128)(2,1)S(1)} %get-tuple-element.20.pick_ref, bf16[5,2,1280,256]{3,2,1,0:T(8,128)(2,1)S(1)} %bitcast.15), custom_call_target="tpu_custom_call" | custom-call | flops 2500000000 | bytes 12000000 | tf_op jit(solution)/shard_map/receive/pallas_call | solution.py:362
  (1 shorter events, 0.0 us)
Async XLA Ops:
  1.6 6.9 %collective-permute-start = (bf16[16,2560]{1,0:T(8,128)(2,1)S(1)}, bf16[16,2560]{1,0:T(8,128)(2,1)S(1)}, u32[]{:S(2)}, u32[]{:S(2)}) collective-permute-start(bf16[16,2560]{1,0:T(8,128)(2,1)S(1)} %get-tuple-element.17), channel_id=1, source_target_pairs={{0,4},{4,8},{8,12},{12,16},{16,20},{20,24},{24,28},{28,32},{32,36}... | collective-permute-start | bytes 245768 | tf_op jit(solution)/shard_map/ppermute | solution.py:392
  6.5 5.8 %collective-permute-start.1 = (bf16[16,2560]{1,0:T(8,128)(2,1)S(1)}, bf16[16,2560]{1,0:T(8,128)(2,1)S(1)}, u32[]{:S(2)}, u32[]{:S(2)}) collective-permute-start(bf16[16,2560]{1,0:T(8,128)(2,1)S(1)} %get-tuple-element.18), channel_id=1, source_target_pairs={{4,0},{8,4},{12,8},{16,12},{20,16},{24,20},{28,24},{32,28},{36,32}... | collective-permute-start | bytes 245768 | tf_op jit(solution)/shard_map/ppermute | solution.py:393
  12.3 69.3 %copy-start = (bf16[1,3330,1280]{2,1,0:T(8,128)(2,1)S(1)}, bf16[1,3330,1280]{2,1,0:T(8,128)(2,1)}, u32[]{:S(2)}) copy-start(bf16[1,3330,1280]{2,1,0:T(8,128)(2,1)} %legendre_ref.1) | copy-start | bytes 25574404
  21.2 118.2 %slice-start = ((s8[6553600]{0:T(1024)(128)(4,1)}), s8[4194304]{0:T(1024)(128)(4,1)S(1)}, s32[]{:S(2)}) async-start(s8[6553600]{0:T(1024)(128)(4,1)} %bitcast.14), calls=%async_computation.2 | async-start | bytes 8388608
  81.6 57.8 %slice-start.1 = ((s8[6553600]{0:T(1024)(128)(4,1)}), s8[2359296]{0:T(1024)(128)(4,1)S(1)}, s32[]{:S(2)}) async-start(s8[6553600]{0:T(1024)(128)(4,1)} %bitcast.14), calls=%async_computation.3 | async-start | bytes 4718592

commit v5 on v4

--- a/solution.py
+++ b/solution.py
@@ -81,10 +81,8 @@
 
 
 def load_kernel(field_ref, metric_ref, quad_ref, sets_ref, *refs):
-    first_ref, last_ref, field_out, metric_out, quad_out, sets_out, landed = refs
+    field_out, metric_out, quad_out, sets_out, landed = refs
     moves = [
-        (field_ref.at[pl.ds(0, LEVS)], first_ref),
-        (field_ref.at[pl.ds(ROWS - LEVS, LEVS)], last_ref),
         (field_ref, field_out),
         (metric_ref, metric_out),
         (quad_ref, quad_out),
@@ -98,9 +96,7 @@
 
 
 def load(*arrays):
-    field = arrays[0]
-    halo = (LEVS, NLON)
-    shapes = [(halo, field.dtype), (halo, field.dtype)] + [(a.shape, a.dtype) for a in arrays]
+    shapes = [(a.shape, a.dtype) for a in arrays]
     return pl.pallas_call(
         load_kernel,
         out_shape=tuple(pltpu.VMEM(*shape) for shape in shapes),
@@ -118,6 +114,8 @@
     out_ref, pick_ref, halves, mixed, rows, picks, tables, landed,
 ):
     slot = pl.program_id(0)
+    first_lat = lax.axis_index("lat") * BAND
+    lev_index = lax.axis_index("lev")
 
     def fetch(which):
         return pltpu.make_async_copy(table_ref.at[which], tables.at[which], landed.at[which])
@@ -136,7 +134,8 @@
             total = metric_ref[0, lat] * (north - centre) + metric_ref[1, lat] * (south - centre)
             total = total + metric_ref[2, lat] * zonal
             first, second = total[:, :HALF], total[:, HALF:]
-            where = pl.ds(pl.multiple_of(lat * LEVS, LEVS), LEVS)
+            place = 4 * (lat // 4) + (lat + lev_index) % 4
+            where = pl.ds(pl.multiple_of(place * LEVS, LEVS), LEVS)
             halves[0, where, :] = (first + second).astype(jnp.bfloat16)
             halves[1, where, :] = (first - second).astype(jnp.bfloat16)
 
@@ -158,20 +157,18 @@
                     pl.ds(lev, LAT_DEVS, stride=LEV_DEVS), :
                 ].astype(jnp.bfloat16)
 
-    first_lat = lax.axis_index("lat") * BAND
-    lev_index = lax.axis_index("lev")
     fetch(slot).wait()
     for odd in range(2):
         waves = jnp.dot(
             halves[(slot + odd) % 2], tables[slot, odd], preferred_element_type=jnp.float32
         )
-        for lat in range(BAND):
+        for place in range(BAND):
+            lat = place // 4 * 4 + (place + LEV_DEVS - lev_index) % 4
             weight = quad_ref[first_lat + lat]
-            weighted = (waves[lat * LEVS : (lat + 1) * LEVS] * weight).astype(jnp.bfloat16)
-            place = 4 * (lat // 4) + (lat + lev_index) % 4
+            weighted = (waves[place * LEVS : (place + 1) * LEVS] * weight).astype(jnp.bfloat16)
             for part in range(2):
-                start = pl.multiple_of((2 * place + part) * LEVS, LEVS)
-                mixed[pl.ds(start, LEVS), odd * 128 : odd * 128 + 128] = weighted[
+                start = (2 * place + part) * LEVS
+                mixed[start : start + LEVS, odd * 128 : odd * 128 + 128] = weighted[
                     :, part * 128 : part * 128 + 128
                 ]
     dealt = lax.dot_general(
@@ -289,7 +286,7 @@
         )
         if slot == SLOTS - 1:
             back = back + jnp.dot(last, tail[...], preferred_element_type=jnp.float32)
-        columns[slot * NLAT : slot * NLAT + NLAT, :] = back.T
+        columns[slot * NLAT : slot * NLAT + NLAT, :] = back.astype(jnp.bfloat16).T.astype(jnp.float32)
         for part in range(5):
             tiles = [
                 rotated(columns[pl.ds(slot * NLAT + 4 * part + group, LAT_DEVS, stride=BAND), :], group)
@@ -338,7 +335,7 @@
             for part in range(5):
                 tile = rows[pl.ds(slot * 5 + part, SETS, stride=PITCH), :]
                 dealt = jnp.dot(
-                    tile.T.astype(jnp.bfloat16), pick_ref[...], preferred_element_type=jnp.float32
+                    tile.astype(jnp.bfloat16).T, pick_ref[...], preferred_element_type=jnp.float32
                 ).astype(jnp.bfloat16)
                 for group in range(8):
                     lat, side = 4 * part + (group // 2 + LEV_DEVS - lev_index) % 4, group % 2
@@ -388,9 +385,9 @@
     field = jnp.transpose(field, (1, 0, 2)).reshape(ROWS, NLON)
     forward = [(i, i + 1) for i in range(LAT_DEVS - 1)]
     backward = [(i + 1, i) for i in range(LAT_DEVS - 1)]
-    first, last, field, metric, quad, sets = load(field, metric, quad_weight, assignment.T)
-    north = lax.ppermute(last, "lat", forward)
-    south = lax.ppermute(first, "lat", backward)
+    north = lax.ppermute(field[ROWS - LEVS :], "lat", forward)
+    south = lax.ppermute(field[:LEVS], "lat", backward)
+    field, metric, quad, sets = load(field, metric, quad_weight, assignment.T)
     message, pick = send(metric, quad, sets, field, north, south, forward_table())
     back = exchange(spectral(sets, exchange(message), legendre))
     out = receive(back, pick, inverse_table())

time: 145 us -> 143 us (0.986)
  waiting for transfers between devices: 3.82 us -> 0.01 us
  blocking collectives: 111 us -> 113 us
    ppermute x2, waiting for transfers between devices: 3.82 us -> 0.01 us  [the longest x1 0.01 us: per_device(): south = lax.ppermute(field[:LEVS], 'lat', backward)]
    all_to_all x2, blocking collectives: 111 us -> 113 us  [exchange(): lax.all_to_all(pairs, AXES, split_axis=0, concat_axis=0, tiled=True)]
  transfers between devices with their start and end apart: 2 -> 2, of which waited for: 1 -> 0; matrix products, arithmetic and copies ran while one was open for 0% -> 0% of each run, Pallas kernels for 0% -> 1%
where the time goes in v5:
time: 143 us
  blocking collectives  113 us (79%)
  Pallas kernels  21.6 us (15%)
  starting transfers between devices  7.07 us (5%)
    all_to_all x2, blocking collectives, exchange(): lax.all_to_all(pairs, AXES, split_axis=0, concat_axis=0, tiled=True)  113 us
    pallas_call x1, Pallas kernels, send(): pl.pallas_call(send_kernel, out_shape=(jax.ShapeDtypeStruct((MSG_ROWS, 12...  8.5 us
    pallas_call x1, Pallas kernels, spectral(): pl.pallas_call(spectral_kernel, out_shape=jax.ShapeDtypeStruct((MSG_ROWS,...  6.39 us
    pallas_call x1, Pallas kernels, receive(): pl.pallas_call(receive_kernel, out_shape=jax.ShapeDtypeStruct((ROWS, NLON...  5.24 us
    ppermute x1, starting transfers between devices, per_device(): south = lax.ppermute(field[:LEVS], 'lat', backward)  5.15 us
  transfers between devices with their start and end apart: 2, of which 0 were waited for; matrix products, arithmetic and copies ran while one was open for 0% of the time, Pallas kernels for 1%

profile of v5, /device:TPU:1, one launch (start us, length us, event | category | flops | bytes accessed | tf_op | source)
XLA Modules:
  0.0 142.7 jit_solution(10033107069976139959)
XLA Ops:
  0.0 0.9 slice_bitcast_fusion
  0.9 5.1 %collective-permute-start.1 = (bf16[16,2560]{1,0:T(8,128)(2,1)S(1)}, bf16[16,2560]{1,0:T(8,128)(2,1)S(1)}, u32[]{:S(2)}, u32[]{:S(2)}) collective-permute-start(bf16[16,2560]{1,0:T(8,128)(2,1)S(1)} %get-tuple-element.17), channel_id=1, source_target_pairs={{4,0},{8,4},{12,8},{16,12},{20,16},{24,20},{28,24},{32,28},{36,32}... | collective-permute-start | bytes 245768 | tf_op jit(solution)/shard_map/ppermute | solution.py:389
  6.1 1.9 %collective-permute-start = (bf16[16,2560]{1,0:T(8,128)(2,1)S(1)}, bf16[16,2560]{1,0:T(8,128)(2,1)S(1)}, u32[]{:S(2)}, u32[]{:S(2)}) collective-permute-start(bf16[16,2560]{1,0:T(8,128)(2,1)S(1)} %get-tuple-element.18), channel_id=1, source_target_pairs={{0,4},{4,8},{8,12},{12,16},{16,20},{20,24},{24,28},{28,32},{32,36}... | collective-permute-start | bytes 245768 | tf_op jit(solution)/shard_map/ppermute | solution.py:388
  8.0 1.5 %load.1 = (bf16[320,2560]{1,0:T(8,128)(2,1)S(1)}, f32[3,20]{1,0:T(4,128)S(1)}, f32[1280]{0:T(1024)S(1)}, s32[5,256]{1,0:T(8,128)S(1)}) custom-call(bf16[320,2560]{1,0:T(8,128)(2,1)} %bitcast.22, f32[3,20]{1,0:T(4,128)} %metric_ref.1, f32[1280]{0:T(1024)} %quad_ref.1, s32[5,256]{1,0:T(8,128)} %bitcast.23), custom_call_target="tpu_custom_call" | custom-call | bytes 4000000 | tf_op jit(solution)/shard_map/load/pallas_call | solution.py:100
  9.5 0.0 collective-permute-done.1.south_ref
  9.5 0.0 collective-permute-done.north_ref
  9.5 0.0 copy-start
  9.5 8.5 %send.1 = (bf16[6656,128]{1,0:T(8,128)(2,1)S(1)}, bf16[256,256]{1,0:T(8,128)(2,1)S(1)}) custom-call(f32[3,20]{1,0:T(4,128)S(1)} %get-tuple-element.12.metric_ref, f32[1280]{0:T(1024)S(1)} %get-tuple-element.13.quad_ref, s32[5,256]{1,0:T(8,128)S(1)} %get-tuple-element.11.sets_ref, bf16[320,2560]{1,0:T(8,128)(2,1)S(1)} %get-tuple-element.14.field_ref, ...), custom_call_target="tpu_custom_call" | custom-call | flops 2500000000 | bytes 12000000 | tf_op jit(solution)/shard_map/send/pallas_call | solution.py:191
  18.0 0.0 slice-start
  18.1 62.2 %all_to_all.10 = bf16[256,13,2,128]{3,2,1,0:T(2,128)(2,1)S(1)} all-to-all(bf16[256,13,2,128]{3,2,1,0:T(2,128)(2,1)S(1)} %bitcast.20), channel_id=1, replica_groups=mesh['lat'=64,'lev'=4] {'lev','lat'}, dimensions={0} | all-to-all | bytes 3407872 | tf_op jit(solution)/shard_map/all_to_all | solution.py:381
  80.3 0.0 copy-done
  80.3 0.0 slice-start.1
  80.3 6.4 %spectral.1 = bf16[6656,128]{1,0:T(8,128)(2,1)S(1)} custom-call(s32[5,256]{1,0:T(8,128)S(1)} %get-tuple-element.11.sets_ref, bf16[6656,128]{1,0:T(8,128)(2,1)S(1)} %bitcast.16, bf16[1,3330,1280]{2,1,0:T(8,128)(2,1)S(1)} %copy-done), custom_call_target="tpu_custom_call" | custom-call | flops 2500000000 | bytes 12000000 | tf_op jit(solution)/shard_map/spectral/pallas_call | solution.py:303
  86.7 50.8 %all_to_all.11 = bf16[256,13,2,128]{3,2,1,0:T(2,128)(2,1)S(1)} all-to-all(bf16[256,13,2,128]{3,2,1,0:T(2,128)(2,1)S(1)} %bitcast.17), channel_id=1, replica_groups=mesh['lat'=64,'lev'=4] {'lev','lat'}, dimensions={0} | all-to-all | bytes 3407872 | tf_op jit(solution)/shard_map/all_to_all | solution.py:381
  137.5 0.0 slice-done
  137.5 0.0 slice-done.1
  137.5 5.2 %receive.1 = bf16[320,2560]{1,0:T(8,128)(2,1)} custom-call(bf16[6656,128]{1,0:T(8,128)(2,1)S(1)} %bitcast.15, bf16[256,256]{1,0:T(8,128)(2,1)S(1)} %get-tuple-element.16.pick_ref, bf16[5,2,1280,256]{3,2,1,0:T(8,128)(2,1)S(1)} %bitcast.19), custom_call_target="tpu_custom_call" | custom-call | flops 2500000000 | bytes 12000000 | tf_op jit(solution)/shard_map/receive/pallas_call | solution.py:359
  (1 shorter events, 0.0 us)
Async XLA Ops:
  0.9 8.6 %collective-permute-start.1 = (bf16[16,2560]{1,0:T(8,128)(2,1)S(1)}, bf16[16,2560]{1,0:T(8,128)(2,1)S(1)}, u32[]{:S(2)}, u32[]{:S(2)}) collective-permute-start(bf16[16,2560]{1,0:T(8,128)(2,1)S(1)} %get-tuple-element.17), channel_id=1, source_target_pairs={{4,0},{8,4},{12,8},{16,12},{20,16},{24,20},{28,24},{32,28},{36,32}... | collective-permute-start | bytes 245768 | tf_op jit(solution)/shard_map/ppermute | solution.py:389
  6.1 3.4 %collective-permute-start = (bf16[16,2560]{1,0:T(8,128)(2,1)S(1)}, bf16[16,2560]{1,0:T(8,128)(2,1)S(1)}, u32[]{:S(2)}, u32[]{:S(2)}) collective-permute-start(bf16[16,2560]{1,0:T(8,128)(2,1)S(1)} %get-tuple-element.18), channel_id=1, source_target_pairs={{0,4},{4,8},{8,12},{12,16},{16,20},{20,24},{24,28},{28,32},{32,36}... | collective-permute-start | bytes 245768 | tf_op jit(solution)/shard_map/ppermute | solution.py:388
  9.5 70.8 %copy-start = (bf16[1,3330,1280]{2,1,0:T(8,128)(2,1)S(1)}, bf16[1,3330,1280]{2,1,0:T(8,128)(2,1)}, u32[]{:S(2)}) copy-start(bf16[1,3330,1280]{2,1,0:T(8,128)(2,1)} %legendre_ref.1) | copy-start | bytes 25574404
  18.0 119.5 %slice-start = ((s8[6553600]{0:T(1024)(128)(4,1)}), s8[4194304]{0:T(1024)(128)(4,1)S(1)}, s32[]{:S(2)}) async-start(s8[6553600]{0:T(1024)(128)(4,1)} %bitcast.18), calls=%async_computation.2 | async-start | bytes 8388608
  80.3 57.2 %slice-start.1 = ((s8[6553600]{0:T(1024)(128)(4,1)}), s8[2359296]{0:T(1024)(128)(4,1)S(1)}, s32[]{:S(2)}) async-start(s8[6553600]{0:T(1024)(128)(4,1)} %bitcast.18), calls=%async_computation.3 | async-start | bytes 4718592

commit v6 on v5

--- a/solution.py
+++ b/solution.py
@@ -113,101 +113,84 @@
     metric_ref, quad_ref, sets_ref, field_ref, north_ref, south_ref, table_ref,
     out_ref, pick_ref, halves, mixed, rows, picks, tables, landed,
 ):
-    slot = pl.program_id(0)
     first_lat = lax.axis_index("lat") * BAND
     lev_index = lax.axis_index("lev")
 
     def fetch(which):
         return pltpu.make_async_copy(table_ref.at[which], tables.at[which], landed.at[which])
 
-    @pl.when(slot == 0)
-    def _():
-        for which in range(SLOTS):
-            fetch(which).start()
-
-        def band(lat):
-            return field_ref[pl.ds(pl.multiple_of(lat * LEVS, LEVS), LEVS), :].astype(jnp.float32)
-
-        def stencil(lat, north, south):
-            centre = band(lat)
-            zonal = pltpu.roll(centre, 1, 1) + pltpu.roll(centre, NLON - 1, 1) - 2.0 * centre
-            total = metric_ref[0, lat] * (north - centre) + metric_ref[1, lat] * (south - centre)
-            total = total + metric_ref[2, lat] * zonal
-            first, second = total[:, :HALF], total[:, HALF:]
-            place = 4 * (lat // 4) + (lat + lev_index) % 4
-            where = pl.ds(pl.multiple_of(place * LEVS, LEVS), LEVS)
-            halves[0, where, :] = (first + second).astype(jnp.bfloat16)
-            halves[1, where, :] = (first - second).astype(jnp.bfloat16)
-
-        stencil(0, north_ref[...].astype(jnp.float32), band(1))
-        stencil(BAND - 1, band(BAND - 2), south_ref[...].astype(jnp.float32))
-
-        @pl.loop(1, BAND - 1)
-        def _(lat):
-            stencil(lat, band(lat - 1), band(lat + 1))
-
-        sets = sets_ref[0:1, :]
-        position = (sets % 2) * (SETS // 2) + sets // 2
-        spots = lax.broadcasted_iota(jnp.int32, (SETS, SETS), 0)
+    for which in range(SLOTS):
+        fetch(which).start()
+
+    def band(lat):
+        return field_ref[pl.ds(pl.multiple_of(lat * LEVS, LEVS), LEVS), :].astype(jnp.float32)
+
+    def stencil(lat, north, south):
+        centre = band(lat)
+        zonal = pltpu.roll(centre, 1, 1) + pltpu.roll(centre, NLON - 1, 1) - 2.0 * centre
+        total = metric_ref[0, lat] * (north - centre) + metric_ref[1, lat] * (south - centre)
+        total = total + metric_ref[2, lat] * zonal
+        first, second = total[:, :HALF], total[:, HALF:]
+        place = 4 * (lat // 4) + (lat + lev_index) % 4
+        where = pl.ds(pl.multiple_of(place * LEVS, LEVS), LEVS)
+        halves[0, where, :] = (first + second).astype(jnp.bfloat16)
+        halves[1, where, :] = (first - second).astype(jnp.bfloat16)
+
+    stencil(0, north_ref[...].astype(jnp.float32), band(1))
+    stencil(BAND - 1, band(BAND - 2), south_ref[...].astype(jnp.float32))
+
+    @pl.loop(1, BAND - 1)
+    def _(lat):
+        stencil(lat, band(lat - 1), band(lat + 1))
+
+    sets = sets_ref[0:1, :]
+    position = (sets % 2) * (SETS // 2) + sets // 2
+    spots = lax.broadcasted_iota(jnp.int32, (SETS, SETS), 0)
+    for odd in range(2):
+        one_hot = jnp.where(spots[odd * 128 : odd * 128 + 128] == position, 1.0, 0.0)
+        picks[...] = one_hot.T
+        for lev in range(LEV_DEVS):
+            pick_ref[lev * LAT_DEVS : (lev + 1) * LAT_DEVS, odd * 128 : odd * 128 + 128] = picks[
+                pl.ds(lev, LAT_DEVS, stride=LEV_DEVS), :
+            ].astype(jnp.bfloat16)
+
+    for slot in range(SLOTS):
+        fetch(slot).wait()
         for odd in range(2):
-            one_hot = jnp.where(spots[odd * 128 : odd * 128 + 128] == position, 1.0, 0.0)
-            picks[...] = one_hot.T
-            for lev in range(LEV_DEVS):
-                pick_ref[lev * LAT_DEVS : (lev + 1) * LAT_DEVS, odd * 128 : odd * 128 + 128] = picks[
-                    pl.ds(lev, LAT_DEVS, stride=LEV_DEVS), :
-                ].astype(jnp.bfloat16)
-
-    fetch(slot).wait()
-    for odd in range(2):
-        waves = jnp.dot(
-            halves[(slot + odd) % 2], tables[slot, odd], preferred_element_type=jnp.float32
+            waves = jnp.dot(
+                halves[(slot + odd) % 2], tables[slot, odd], preferred_element_type=jnp.float32
+            )
+            for place in range(BAND):
+                lat = place // 4 * 4 + (place + LEV_DEVS - lev_index) % 4
+                weight = quad_ref[first_lat + lat]
+                weighted = (waves[place * LEVS : (place + 1) * LEVS] * weight).astype(jnp.bfloat16)
+                for part in range(2):
+                    start = (2 * place + part) * LEVS
+                    mixed[slot, start : start + LEVS, odd * 128 : odd * 128 + 128] = weighted[
+                        :, part * 128 : part * 128 + 128
+                    ]
+        dealt = lax.dot_general(
+            pick_ref[...], mixed[slot], (((1,), (1,)), ((), ())), preferred_element_type=jnp.float32
         )
-        for place in range(BAND):
-            lat = place // 4 * 4 + (place + LEV_DEVS - lev_index) % 4
-            weight = quad_ref[first_lat + lat]
-            weighted = (waves[place * LEVS : (place + 1) * LEVS] * weight).astype(jnp.bfloat16)
-            for part in range(2):
-                start = (2 * place + part) * LEVS
-                mixed[start : start + LEVS, odd * 128 : odd * 128 + 128] = weighted[
-                    :, part * 128 : part * 128 + 128
-                ]
-    dealt = lax.dot_general(
-        pick_ref[...], mixed[...], (((1,), (1,)), ((), ())), preferred_element_type=jnp.float32
-    )
-    for part in range(5):
-        rows[pl.ds(slot * 5 + part, SETS, stride=PITCH), :] = dealt[:, part * 128 : part * 128 + 128]
-
-    @pl.when(slot == SLOTS - 1)
-    def _():
-        copy_rows(out_ref, rows)
+        for part in range(5):
+            rows[pl.ds(slot * 5 + part, SETS, stride=PITCH), :] = dealt[:, part * 128 : part * 128 + 128]
+    copy_rows(out_ref, rows)
 
 
 def send(metric, quad, sets, field, north, south, table):
     smem = pl.BlockSpec(memory_space=pltpu.SMEM)
-
-    def whole(*shape):
-        return pl.BlockSpec(shape, lambda i: (0,) * len(shape))
-
+    vmem = pl.BlockSpec(memory_space=pltpu.VMEM)
     return pl.pallas_call(
         send_kernel,
         out_shape=(
             jax.ShapeDtypeStruct((MSG_ROWS, 128), jnp.bfloat16),
             jax.ShapeDtypeStruct((SETS, SETS), jnp.bfloat16),
         ),
-        grid=(SLOTS,),
-        in_specs=[
-            smem,
-            smem,
-            whole(SLOTS, SETS),
-            whole(ROWS, NLON),
-            whole(LEVS, NLON),
-            whole(LEVS, NLON),
-            pl.BlockSpec(memory_space=pltpu.HBM),
-        ],
-        out_specs=(whole(MSG_ROWS, 128), whole(SETS, SETS)),
+        in_specs=[smem, smem, vmem, vmem, vmem, vmem, pl.BlockSpec(memory_space=pltpu.HBM)],
+        out_specs=(vmem, vmem),
         scratch_shapes=[
             pltpu.VMEM((2, ROWS, HALF), jnp.bfloat16),
-            pltpu.VMEM((2 * ROWS, SETS), jnp.bfloat16),
+            pltpu.VMEM((SLOTS, 2 * ROWS, SETS), jnp.bfloat16),
             pltpu.VMEM((MSG_ROWS, 128), jnp.float32),
             pltpu.VMEM((SETS, 128), jnp.float32),
             pltpu.VMEM((SLOTS, 2, HALF, SETS), jnp.bfloat16),
@@ -324,48 +307,40 @@
 
 
 def receive_kernel(got_ref, pick_ref, table_ref, out_ref, rows, waves):
-    block = pl.program_id(0)
     lev_index = lax.axis_index("lev")
-
-    @pl.when(block == 0)
-    def _():
-        copy_rows(rows, got_ref)
-
-        for slot in range(SLOTS):
-            for part in range(5):
-                tile = rows[pl.ds(slot * 5 + part, SETS, stride=PITCH), :]
-                dealt = jnp.dot(
-                    tile.astype(jnp.bfloat16).T, pick_ref[...], preferred_element_type=jnp.float32
-                ).astype(jnp.bfloat16)
-                for group in range(8):
-                    lat, side = 4 * part + (group // 2 + LEV_DEVS - lev_index) % 4, group % 2
-                    row = pl.multiple_of(lat * LEVS, LEVS)
-                    for parity in range(2):
-                        odd = (slot + parity) % 2
-                        place = (2 * slot + side) * 128
-                        waves[parity, pl.ds(row, LEVS), place : place + 128] = dealt[
-                            group * LEVS : group * LEVS + LEVS, odd * 128 : odd * 128 + 128
-                        ]
-
-    even = jnp.dot(waves[0], table_ref[0, 0], preferred_element_type=jnp.float32)
-    odd = jnp.dot(waves[1], table_ref[0, 1], preferred_element_type=jnp.float32)
-    first = pl.multiple_of(block * SETS, SETS)
-    out_ref[:, pl.ds(first, SETS)] = (even + odd).astype(jnp.bfloat16)
-    second = pl.multiple_of(HALF + block * SETS, SETS)
-    out_ref[:, pl.ds(second, SETS)] = (even - odd).astype(jnp.bfloat16)
+    copy_rows(rows, got_ref)
+
+    for slot in range(SLOTS):
+        for part in range(5):
+            tile = rows[pl.ds(slot * 5 + part, SETS, stride=PITCH), :]
+            dealt = jnp.dot(
+                tile.astype(jnp.bfloat16).T, pick_ref[...], preferred_element_type=jnp.float32
+            ).astype(jnp.bfloat16)
+            for group in range(8):
+                lat, side = 4 * part + (group // 2 + LEV_DEVS - lev_index) % 4, group % 2
+                row = pl.multiple_of(lat * LEVS, LEVS)
+                for parity in range(2):
+                    odd = (slot + parity) % 2
+                    place = (2 * slot + side) * 128
+                    waves[parity, pl.ds(row, LEVS), place : place + 128] = dealt[
+                        group * LEVS : group * LEVS + LEVS, odd * 128 : odd * 128 + 128
+                    ]
+
+    for block in range(SLOTS):
+        even = jnp.dot(waves[0], table_ref[block, 0], preferred_element_type=jnp.float32)
+        odd = jnp.dot(waves[1], table_ref[block, 1], preferred_element_type=jnp.float32)
+        first, second = block * SETS, HALF + block * SETS
+        out_ref[:, first : first + SETS] = (even + odd).astype(jnp.bfloat16)
+        out_ref[:, second : second + SETS] = (even - odd).astype(jnp.bfloat16)
 
 
 def receive(got, pick, table):
+    vmem = pl.BlockSpec(memory_space=pltpu.VMEM)
     return pl.pallas_call(
         receive_kernel,
         out_shape=jax.ShapeDtypeStruct((ROWS, NLON), jnp.bfloat16),
-        grid=(SLOTS,),
-        in_specs=[
-            pl.BlockSpec((MSG_ROWS, 128), lambda i: (0, 0)),
-            pl.BlockSpec((SETS, SETS), lambda i: (0, 0)),
-            pl.BlockSpec((1, 2, HALF, SETS), lambda i: (i, 0, 0, 0)),
-        ],
-        out_specs=pl.BlockSpec((ROWS, NLON), lambda i: (0, 0)),
+        in_specs=[vmem, vmem, vmem],
+        out_specs=vmem,
         scratch_shapes=[
             pltpu.VMEM((MSG_ROWS, 128), jnp.float32),
             pltpu.VMEM((2, ROWS, HALF), jnp.bfloat16),

time: 143 us -> 142 us (level)
  no operation moved by 1% of the time
where the time goes in v6:
time: 142 us
  blocking collectives  113 us (80%)
  Pallas kernels  20.5 us (14%)
  starting transfers between devices  7.07 us (5%)
    all_to_all x2, blocking collectives, exchange(): lax.all_to_all(pairs, AXES, split_axis=0, concat_axis=0, tiled=True)  113 us
    pallas_call x1, Pallas kernels, send(): pl.pallas_call(send_kernel, out_shape=(jax.ShapeDtypeStruct((MSG_ROWS, 12...  8.17 us
    pallas_call x1, Pallas kernels, spectral(): pl.pallas_call(spectral_kernel, out_shape=jax.ShapeDtypeStruct((MSG_ROWS,...  6.39 us
    ppermute x1, starting transfers between devices, per_device(): south = lax.ppermute(field[:LEVS], 'lat', backward)  5.15 us
    pallas_call x1, Pallas kernels, receive(): pl.pallas_call(receive_kernel, out_shape=jax.ShapeDtypeStruct((ROWS, NLON...  4.42 us
  transfers between devices with their start and end apart: 2, of which 0 were waited for; matrix products, arithmetic and copies ran while one was open for 0% of the time, Pallas kernels for 1%

profile of v6, /device:TPU:1, one launch (start us, length us, event | category | flops | bytes accessed | tf_op | source)
XLA Modules:
  0.0 141.6 jit_solution(17421108740724171794)
XLA Ops:
  0.0 0.9 slice_bitcast_fusion
  0.9 5.1 %collective-permute-start.1 = (bf16[16,2560]{1,0:T(8,128)(2,1)S(1)}, bf16[16,2560]{1,0:T(8,128)(2,1)S(1)}, u32[]{:S(2)}, u32[]{:S(2)}) collective-permute-start(bf16[16,2560]{1,0:T(8,128)(2,1)S(1)} %get-tuple-element.17), channel_id=1, source_target_pairs={{4,0},{8,4},{12,8},{16,12},{20,16},{24,20},{28,24},{32,28},{36,32}... | collective-permute-start | bytes 245768 | tf_op jit(solution)/shard_map/ppermute | solution.py:364
  6.1 1.9 %collective-permute-start = (bf16[16,2560]{1,0:T(8,128)(2,1)S(1)}, bf16[16,2560]{1,0:T(8,128)(2,1)S(1)}, u32[]{:S(2)}, u32[]{:S(2)}) collective-permute-start(bf16[16,2560]{1,0:T(8,128)(2,1)S(1)} %get-tuple-element.18), channel_id=1, source_target_pairs={{0,4},{4,8},{8,12},{12,16},{16,20},{20,24},{24,28},{28,32},{32,36}... | collective-permute-start | bytes 245768 | tf_op jit(solution)/shard_map/ppermute | solution.py:363
  8.0 1.5 %load.1 = (bf16[320,2560]{1,0:T(8,128)(2,1)S(1)}, f32[3,20]{1,0:T(4,128)S(1)}, f32[1280]{0:T(1024)S(1)}, s32[5,256]{1,0:T(8,128)S(1)}) custom-call(bf16[320,2560]{1,0:T(8,128)(2,1)} %bitcast.22, f32[3,20]{1,0:T(4,128)} %metric_ref.1, f32[1280]{0:T(1024)} %quad_ref.1, s32[5,256]{1,0:T(8,128)} %bitcast.23), custom_call_target="tpu_custom_call" | custom-call | bytes 4000000 | tf_op jit(solution)/shard_map/load/pallas_call | solution.py:100
  9.5 0.0 collective-permute-done.1.south_ref
  9.5 0.0 collective-permute-done.north_ref
  9.5 0.0 copy-start
  9.5 8.2 %send.1 = (bf16[6656,128]{1,0:T(8,128)(2,1)S(1)}, bf16[256,256]{1,0:T(8,128)(2,1)S(1)}) custom-call(f32[3,20]{1,0:T(4,128)S(1)} %get-tuple-element.12.metric_ref, f32[1280]{0:T(1024)S(1)} %get-tuple-element.13.quad_ref, s32[5,256]{1,0:T(8,128)S(1)} %get-tuple-element.11.sets_ref, bf16[320,2560]{1,0:T(8,128)(2,1)S(1)} %get-tuple-element.14.field_ref, ...), custom_call_target="tpu_custom_call" | custom-call | flops 2500000000 | bytes 12000000 | tf_op jit(solution)/shard_map/send/pallas_call | solution.py:183
  17.7 0.0 slice-start
  17.7 62.3 %all_to_all.10 = bf16[256,13,2,128]{3,2,1,0:T(2,128)(2,1)S(1)} all-to-all(bf16[256,13,2,128]{3,2,1,0:T(2,128)(2,1)S(1)} %bitcast.20), channel_id=1, replica_groups=mesh['lat'=64,'lev'=4] {'lev','lat'}, dimensions={0} | all-to-all | bytes 3407872 | tf_op jit(solution)/shard_map/all_to_all | solution.py:356
  80.0 0.0 copy-done
  80.0 0.0 slice-start.1
  80.0 6.4 %spectral.1 = bf16[6656,128]{1,0:T(8,128)(2,1)S(1)} custom-call(s32[5,256]{1,0:T(8,128)S(1)} %get-tuple-element.11.sets_ref, bf16[6656,128]{1,0:T(8,128)(2,1)S(1)} %bitcast.16, bf16[1,3330,1280]{2,1,0:T(8,128)(2,1)S(1)} %copy-done), custom_call_target="tpu_custom_call" | custom-call | flops 2500000000 | bytes 12000000 | tf_op jit(solution)/shard_map/spectral/pallas_call | solution.py:286
  86.4 50.8 %all_to_all.11 = bf16[256,13,2,128]{3,2,1,0:T(2,128)(2,1)S(1)} all-to-all(bf16[256,13,2,128]{3,2,1,0:T(2,128)(2,1)S(1)} %bitcast.17), channel_id=1, replica_groups=mesh['lat'=64,'lev'=4] {'lev','lat'}, dimensions={0} | all-to-all | bytes 3407872 | tf_op jit(solution)/shard_map/all_to_all | solution.py:356
  137.2 0.0 slice-done
  137.2 0.0 slice-done.1
  137.2 4.4 %receive.1 = bf16[320,2560]{1,0:T(8,128)(2,1)} custom-call(bf16[6656,128]{1,0:T(8,128)(2,1)S(1)} %bitcast.15, bf16[256,256]{1,0:T(8,128)(2,1)S(1)} %get-tuple-element.16.pick_ref, bf16[5,2,1280,256]{3,2,1,0:T(8,128)(2,1)S(1)} %bitcast.19), custom_call_target="tpu_custom_call" | custom-call | flops 2500000000 | bytes 12000000 | tf_op jit(solution)/shard_map/receive/pallas_call | solution.py:339
  (1 shorter events, 0.0 us)
Async XLA Ops:
  0.9 8.6 %collective-permute-start.1 = (bf16[16,2560]{1,0:T(8,128)(2,1)S(1)}, bf16[16,2560]{1,0:T(8,128)(2,1)S(1)}, u32[]{:S(2)}, u32[]{:S(2)}) collective-permute-start(bf16[16,2560]{1,0:T(8,128)(2,1)S(1)} %get-tuple-element.17), channel_id=1, source_target_pairs={{4,0},{8,4},{12,8},{16,12},{20,16},{24,20},{28,24},{32,28},{36,32}... | collective-permute-start | bytes 245768 | tf_op jit(solution)/shard_map/ppermute | solution.py:364
  6.1 3.4 %collective-permute-start = (bf16[16,2560]{1,0:T(8,128)(2,1)S(1)}, bf16[16,2560]{1,0:T(8,128)(2,1)S(1)}, u32[]{:S(2)}, u32[]{:S(2)}) collective-permute-start(bf16[16,2560]{1,0:T(8,128)(2,1)S(1)} %get-tuple-element.18), channel_id=1, source_target_pairs={{0,4},{4,8},{8,12},{12,16},{16,20},{20,24},{24,28},{28,32},{32,36}... | collective-permute-start | bytes 245768 | tf_op jit(solution)/shard_map/ppermute | solution.py:363
  9.5 70.5 %copy-start = (bf16[1,3330,1280]{2,1,0:T(8,128)(2,1)S(1)}, bf16[1,3330,1280]{2,1,0:T(8,128)(2,1)}, u32[]{:S(2)}) copy-start(bf16[1,3330,1280]{2,1,0:T(8,128)(2,1)} %legendre_ref.1) | copy-start | bytes 25574404
  17.7 119.5 %slice-start = ((s8[6553600]{0:T(1024)(128)(4,1)}), s8[4194304]{0:T(1024)(128)(4,1)S(1)}, s32[]{:S(2)}) async-start(s8[6553600]{0:T(1024)(128)(4,1)} %bitcast.18), calls=%async_computation.2 | async-start | bytes 8388608
  80.0 57.2 %slice-start.1 = ((s8[6553600]{0:T(1024)(128)(4,1)}), s8[2359296]{0:T(1024)(128)(4,1)S(1)}, s32[]{:S(2)}) async-start(s8[6553600]{0:T(1024)(128)(4,1)} %bitcast.18), calls=%async_computation.3 | async-start | bytes 4718592

commit v7 on v6

--- a/solution.py
+++ b/solution.py
@@ -311,11 +311,15 @@
     copy_rows(rows, got_ref)
 
     for slot in range(SLOTS):
+        tiles = [
+            rows[pl.ds(slot * 5 + part, SETS, stride=PITCH), :].astype(jnp.bfloat16).T
+            for part in range(5)
+        ]
+        joined = jnp.dot(
+            jnp.concatenate(tiles, axis=0), pick_ref[...], preferred_element_type=jnp.float32
+        ).astype(jnp.bfloat16)
         for part in range(5):
-            tile = rows[pl.ds(slot * 5 + part, SETS, stride=PITCH), :]
-            dealt = jnp.dot(
-                tile.astype(jnp.bfloat16).T, pick_ref[...], preferred_element_type=jnp.float32
-            ).astype(jnp.bfloat16)
+            dealt = joined[part * 128 : part * 128 + 128]
             for group in range(8):
                 lat, side = 4 * part + (group // 2 + LEV_DEVS - lev_index) % 4, group % 2
                 row = pl.multiple_of(lat * LEVS, LEVS)

time: 142 us -> 142 us (level)
  no operation moved by 1% of the time
where the time goes in v7:
time: 142 us
  blocking collectives  113 us (80%)
  Pallas kernels  20.6 us (15%)
  starting transfers between devices  7.07 us (5%)
    all_to_all x2, blocking collectives, exchange(): lax.all_to_all(pairs, AXES, split_axis=0, concat_axis=0, tiled=True)  113 us
    pallas_call x1, Pallas kernels, send(): pl.pallas_call(send_kernel, out_shape=(jax.ShapeDtypeStruct((MSG_ROWS, 12...  8.17 us
    pallas_call x1, Pallas kernels, spectral(): pl.pallas_call(spectral_kernel, out_shape=jax.ShapeDtypeStruct((MSG_ROWS,...  6.39 us
    ppermute x1, starting transfers between devices, per_device(): south = lax.ppermute(field[:LEVS], 'lat', backward)  5.15 us
    pallas_call x1, Pallas kernels, receive(): pl.pallas_call(receive_kernel, out_shape=jax.ShapeDtypeStruct((ROWS, NLON...  4.53 us
  transfers between devices with their start and end apart: 2, of which 0 were waited for; matrix products, arithmetic and copies ran while one was open for 0% of the time, Pallas kernels for 1%

profile of v7, /device:TPU:1, one launch (start us, length us, event | category | flops | bytes accessed | tf_op | source)
XLA Modules:
  0.0 141.7 jit_solution(9066730048831862198)
XLA Ops:
  0.0 0.9 slice_bitcast_fusion
  0.9 5.1 %collective-permute-start.1 = (bf16[16,2560]{1,0:T(8,128)(2,1)S(1)}, bf16[16,2560]{1,0:T(8,128)(2,1)S(1)}, u32[]{:S(2)}, u32[]{:S(2)}) collective-permute-start(bf16[16,2560]{1,0:T(8,128)(2,1)S(1)} %get-tuple-element.17), channel_id=1, source_target_pairs={{4,0},{8,4},{12,8},{16,12},{20,16},{24,20},{28,24},{32,28},{36,32}... | collective-permute-start | bytes 245768 | tf_op jit(solution)/shard_map/ppermute | solution.py:368
  6.1 1.9 %collective-permute-start = (bf16[16,2560]{1,0:T(8,128)(2,1)S(1)}, bf16[16,2560]{1,0:T(8,128)(2,1)S(1)}, u32[]{:S(2)}, u32[]{:S(2)}) collective-permute-start(bf16[16,2560]{1,0:T(8,128)(2,1)S(1)} %get-tuple-element.18), channel_id=1, source_target_pairs={{0,4},{4,8},{8,12},{12,16},{16,20},{20,24},{24,28},{28,32},{32,36}... | collective-permute-start | bytes 245768 | tf_op jit(solution)/shard_map/ppermute | solution.py:367
  8.0 1.5 %load.1 = (bf16[320,2560]{1,0:T(8,128)(2,1)S(1)}, f32[3,20]{1,0:T(4,128)S(1)}, f32[1280]{0:T(1024)S(1)}, s32[5,256]{1,0:T(8,128)S(1)}) custom-call(bf16[320,2560]{1,0:T(8,128)(2,1)} %bitcast.22, f32[3,20]{1,0:T(4,128)} %metric_ref.1, f32[1280]{0:T(1024)} %quad_ref.1, s32[5,256]{1,0:T(8,128)} %bitcast.23), custom_call_target="tpu_custom_call" | custom-call | bytes 4000000 | tf_op jit(solution)/shard_map/load/pallas_call | solution.py:100
  9.5 0.0 collective-permute-done.1.south_ref
  9.5 0.0 collective-permute-done.north_ref
  9.5 0.0 copy-start
  9.5 8.2 %send.1 = (bf16[6656,128]{1,0:T(8,128)(2,1)S(1)}, bf16[256,256]{1,0:T(8,128)(2,1)S(1)}) custom-call(f32[3,20]{1,0:T(4,128)S(1)} %get-tuple-element.12.metric_ref, f32[1280]{0:T(1024)S(1)} %get-tuple-element.13.quad_ref, s32[5,256]{1,0:T(8,128)S(1)} %get-tuple-element.11.sets_ref, bf16[320,2560]{1,0:T(8,128)(2,1)S(1)} %get-tuple-element.14.field_ref, ...), custom_call_target="tpu_custom_call" | custom-call | flops 2500000000 | bytes 12000000 | tf_op jit(solution)/shard_map/send/pallas_call | solution.py:183
  17.7 0.0 slice-start
  17.7 62.3 %all_to_all.10 = bf16[256,13,2,128]{3,2,1,0:T(2,128)(2,1)S(1)} all-to-all(bf16[256,13,2,128]{3,2,1,0:T(2,128)(2,1)S(1)} %bitcast.20), channel_id=1, replica_groups=mesh['lat'=64,'lev'=4] {'lev','lat'}, dimensions={0} | all-to-all | bytes 3407872 | tf_op jit(solution)/shard_map/all_to_all | solution.py:360
  80.0 0.0 copy-done
  80.0 0.0 slice-start.1
  80.0 6.4 %spectral.1 = bf16[6656,128]{1,0:T(8,128)(2,1)S(1)} custom-call(s32[5,256]{1,0:T(8,128)S(1)} %get-tuple-element.11.sets_ref, bf16[6656,128]{1,0:T(8,128)(2,1)S(1)} %bitcast.16, bf16[1,3330,1280]{2,1,0:T(8,128)(2,1)S(1)} %copy-done), custom_call_target="tpu_custom_call" | custom-call | flops 2500000000 | bytes 12000000 | tf_op jit(solution)/shard_map/spectral/pallas_call | solution.py:286
  86.4 50.8 %all_to_all.11 = bf16[256,13,2,128]{3,2,1,0:T(2,128)(2,1)S(1)} all-to-all(bf16[256,13,2,128]{3,2,1,0:T(2,128)(2,1)S(1)} %bitcast.17), channel_id=1, replica_groups=mesh['lat'=64,'lev'=4] {'lev','lat'}, dimensions={0} | all-to-all | bytes 3407872 | tf_op jit(solution)/shard_map/all_to_all | solution.py:360
  137.2 0.0 slice-done
  137.2 0.0 slice-done.1
  137.2 4.5 %receive.1 = bf16[320,2560]{1,0:T(8,128)(2,1)} custom-call(bf16[6656,128]{1,0:T(8,128)(2,1)S(1)} %bitcast.15, bf16[256,256]{1,0:T(8,128)(2,1)S(1)} %get-tuple-element.16.pick_ref, bf16[5,2,1280,256]{3,2,1,0:T(8,128)(2,1)S(1)} %bitcast.19), custom_call_target="tpu_custom_call" | custom-call | flops 2500000000 | bytes 12000000 | tf_op jit(solution)/shard_map/receive/pallas_call | solution.py:343
  (1 shorter events, 0.0 us)
Async XLA Ops:
  0.9 8.6 %collective-permute-start.1 = (bf16[16,2560]{1,0:T(8,128)(2,1)S(1)}, bf16[16,2560]{1,0:T(8,128)(2,1)S(1)}, u32[]{:S(2)}, u32[]{:S(2)}) collective-permute-start(bf16[16,2560]{1,0:T(8,128)(2,1)S(1)} %get-tuple-element.17), channel_id=1, source_target_pairs={{4,0},{8,4},{12,8},{16,12},{20,16},{24,20},{28,24},{32,28},{36,32}... | collective-permute-start | bytes 245768 | tf_op jit(solution)/shard_map/ppermute | solution.py:368
  6.1 3.4 %collective-permute-start = (bf16[16,2560]{1,0:T(8,128)(2,1)S(1)}, bf16[16,2560]{1,0:T(8,128)(2,1)S(1)}, u32[]{:S(2)}, u32[]{:S(2)}) collective-permute-start(bf16[16,2560]{1,0:T(8,128)(2,1)S(1)} %get-tuple-element.18), channel_id=1, source_target_pairs={{0,4},{4,8},{8,12},{12,16},{16,20},{20,24},{24,28},{28,32},{32,36}... | collective-permute-start | bytes 245768 | tf_op jit(solution)/shard_map/ppermute | solution.py:367
  9.5 70.5 %copy-start = (bf16[1,3330,1280]{2,1,0:T(8,128)(2,1)S(1)}, bf16[1,3330,1280]{2,1,0:T(8,128)(2,1)}, u32[]{:S(2)}) copy-start(bf16[1,3330,1280]{2,1,0:T(8,128)(2,1)} %legendre_ref.1) | copy-start | bytes 25574404
  17.7 119.5 %slice-start = ((s8[6553600]{0:T(1024)(128)(4,1)}), s8[4194304]{0:T(1024)(128)(4,1)S(1)}, s32[]{:S(2)}) async-start(s8[6553600]{0:T(1024)(128)(4,1)} %bitcast.18), calls=%async_computation.2 | async-start | bytes 8388608
  80.0 57.2 %slice-start.1 = ((s8[6553600]{0:T(1024)(128)(4,1)}), s8[2359296]{0:T(1024)(128)(4,1)S(1)}, s32[]{:S(2)}) async-start(s8[6553600]{0:T(1024)(128)(4,1)} %bitcast.18), calls=%async_computation.3 | async-start | bytes 4718592
